TPU v7x, 256 devices: a whole 4x4x8 slice. The times are simulated.
256 devices in a mesh: snap: 16 (over z, x_hi), mesh: 16 (over x_lo, y, core).
Axes of the slice: x: 4 (x_hi: 2, x_lo: 2; x = x_hi * 2 + x_lo), y: 4, z: 8, core: 2. Of those that a mesh axis runs over, the one named last changes fastest.
Arguments:
- snapshots: float32 [49152, 2048], P('mesh', 'snap'), may hold values from -6 to 6
- region_ids: int32 [96, 512], P('mesh'), may hold values from 0 to 7
- conductivity: float32 [8], replicated, may hold values from 0.2 to 5
Outputs:
- gram: float32 [2048, 2048], P('snap', 'mesh')
All inputs are finite; a program needn't handle non-finite values.
Results may differ from a plain program's by a relative error of at most 0.0003.
Values sent between devices are 32-bit elements; how exact they have to be, the bound alone decides.
A program may use at most 128 MiB of HBM per device.

v0:
```python
import functools
import math

import jax
import jax.numpy as jnp
from jax import lax
from jax.experimental import pallas as pl
from jax.experimental.pallas import tpu as pltpu
from jax.sharding import Mesh
from jax.sharding import PartitionSpec as P


def passed_along(value, axis, steps):
    count = lax.axis_size(axis)
    first, last = (max(0, -steps), min(count, count - steps))
    return lax.ppermute(value, axis, [(source, source + steps) for source in range(first, last)])


def weights_of(region_ids, conductivity):
    table = jnp.arange(conductivity.shape[0], dtype=jnp.int32)
    picked = jnp.where(
        region_ids[:, :, None] == table[None, None, :],
        conductivity[None, None, :],
        jnp.zeros((), conductivity.dtype),
    )
    return jnp.sum(picked, axis=-1) / 36.0


def element_terms(field, below, weight):
    lower = jnp.concatenate([field, below[None]], 0)
    padded = jnp.pad(lower, ((0, 0), (0, 1), (0, 0)))
    corner_a = padded[:-1, :-1]
    corner_b = padded[:-1, 1:]
    corner_e = padded[1:, :-1]
    corner_d = padded[1:, 1:]
    scaled = weight[:, :, None]
    to_a = scaled * (4.0 * corner_a + 2.0 * corner_b + 2.0 * corner_e + corner_d)
    to_b = scaled * (2.0 * corner_a + 4.0 * corner_b + corner_e + 2.0 * corner_d)
    to_e = scaled * (2.0 * corner_a + corner_b + 4.0 * corner_e + 2.0 * corner_d)
    to_d = scaled * (corner_a + 2.0 * corner_b + 2.0 * corner_e + 4.0 * corner_d)
    total = jnp.pad(to_a, ((0, 1), (0, 1), (0, 0))) + jnp.pad(to_b, ((0, 1), (1, 0), (0, 0)))
    total = (
        total + jnp.pad(to_e, ((1, 0), (0, 1), (0, 0))) + jnp.pad(to_d, ((1, 0), (1, 0), (0, 0)))
    )
    return total


def contract(left, right):
    return lax.dot_general(
        left,
        right,
        (((0,), (0,)), ((), ())),
        precision=lax.Precision.HIGH,
        preferred_element_type=jnp.float32,
    )


def pairs(count, to):
    return [(i, to(i)) for i in range(count)]


def square_gather(block, axis):
    count, half = lax.axis_size(axis), block.shape[0] // 2
    to_x, to_z = pairs(count, lambda i: i ^ 1), pairs(count, lambda i: i ^ 2)
    x_low = lax.ppermute(block[:half], axis, to_x)
    z_high = lax.ppermute(block[half:], axis, to_z)
    x_high = lax.ppermute(block[half:], axis, to_x)
    z_low = lax.ppermute(block[:half], axis, to_z)
    corner = [lax.ppermute(x_low, axis, to_z), lax.ppermute(z_high, axis, to_x)]
    return [block, [x_low, x_high], [z_low, z_high], corner]


def ring_gather(block, axis):
    count, half = lax.axis_size(axis), block.shape[0] // 2
    up = pairs(count, lambda i: (i + 1) % count)
    down = pairs(count, lambda i: (i - 1) % count)
    left_low = lax.ppermute(block[:half], axis, up)
    right_high = lax.ppermute(block[half:], axis, down)
    left_high = lax.ppermute(block[half:], axis, up)
    right_low = lax.ppermute(block[:half], axis, down)
    far = [lax.ppermute(left_low, axis, up), lax.ppermute(right_high, axis, down)]
    return [block, [left_low, left_high], far, [right_low, right_high]]


def joined(block):
    return jnp.concatenate(block, 0) if isinstance(block, list) else block


def two_bit_xor(a, b):
    both = (a % 2) * (b % 2) + 2 * ((a // 2) * (b // 2))
    return a + b - 2 * both


def owners_kernel(side, tiles, part_ref, out_ref, slots, send_sems, recv_sems):
    me_r, me_c, me_t = lax.axis_index("r"), lax.axis_index("c"), lax.axis_index("mesh")
    halves = tiles // 2
    parity = me_t % 2
    sends = []
    for i in range(halves):
        j = 2 * i + parity
        dest_c = j // side
        dest_t = me_c + side * (j % side)
        to_self = jnp.logical_and(dest_c == me_c, dest_t == me_t)
        copy = pltpu.make_async_remote_copy(
            src_ref=part_ref.at[i],
            dst_ref=slots.at[me_t // 2],
            send_sem=send_sems.at[i],
            recv_sem=recv_sems.at[me_t // 2],
            device_id=(me_r, dest_c, dest_t),
            device_id_type=pl.DeviceIdType.MESH,
        )
        sends.append((copy, to_self, i))

        @pl.when(jnp.logical_not(to_self))
        def _():
            copy.start()

    for copy, to_self, i in sends:

        @pl.when(to_self)
        def _():
            slots[me_t // 2] = part_ref[i]

    incoming = (me_t // side) % 2
    mine = jnp.logical_and(me_t % side == me_c, parity == incoming)
    for source in range(halves):
        arrival = pltpu.make_async_remote_copy(
            src_ref=slots.at[source],
            dst_ref=slots.at[source],
            send_sem=send_sems.at[source],
            recv_sem=recv_sems.at[source],
            device_id=(me_r, me_c, me_t),
            device_id_type=pl.DeviceIdType.MESH,
        )

        @pl.when(jnp.logical_not(jnp.logical_and(mine, me_t // 2 == source)))
        def _():
            arrival.wait_recv()

    for copy, to_self, _ in sends:

        @pl.when(jnp.logical_not(to_self))
        def _():
            copy.wait_send()

    acc = slots[0]
    for source in range(1, halves):
        acc = acc + slots[source]
    out_ref[...] = acc


def scatter_to_owners(blocks, side, tiles):
    width = blocks.shape[-1]
    me_r, me_c, me_t = lax.axis_index("r"), lax.axis_index("c"), lax.axis_index("mesh")
    halves = tiles // 2
    index = jnp.arange(halves, dtype=jnp.int32)

    def pieces(parity):
        j = 2 * index + parity
        return blocks[two_bit_xor(me_c, j // side), (me_r - j % side) % side]

    parity = me_t % 2
    kept = pieces(parity) + lax.ppermute(pieces(1 - parity), "mesh", pairs(tiles, lambda i: i ^ 1))
    return pl.pallas_call(
        functools.partial(owners_kernel, side, tiles),
        out_shape=jax.ShapeDtypeStruct((width, width), jnp.float32),
        in_specs=[pl.BlockSpec(memory_space=pltpu.VMEM)],
        out_specs=pl.BlockSpec(memory_space=pltpu.VMEM),
        scratch_shapes=[
            pltpu.VMEM((halves, width, width), jnp.float32),
            pltpu.SemaphoreType.DMA((halves,)),
            pltpu.SemaphoreType.DMA((halves,)),
        ],
        compiler_params=pltpu.CompilerParams(has_side_effects=True),
    )(kept)


def local(snapshots, region_ids, conductivity):
    strip, width = region_ids.shape
    node_rows, group_cols = snapshots.shape
    side = lax.axis_size("c")
    tiles = lax.axis_size("mesh")
    field = snapshots.reshape(strip, width, group_cols)
    weight = weights_of(region_ids, conductivity)
    below = passed_along(field[0], "mesh", -1)
    total = element_terms(field, below, weight)
    carried = passed_along(total[strip, :width], "mesh", 1)
    inner = total[:strip, :width]
    panel = jnp.concatenate([inner[:1] + carried[None], inner[1:]], 0).reshape(
        node_rows, group_cols
    )
    rows = square_gather(panel, "c")
    cols = ring_gather(snapshots, "r")
    blocks = jnp.stack(
        [jnp.stack([contract(joined(a), joined(b)) for b in cols], 0) for a in rows], 0
    )
    placed = scatter_to_owners(blocks, side, tiles)
    total_nodes = node_rows * tiles
    return placed / math.sqrt(total_nodes)


def solution(mesh):
    snap = mesh.shape["snap"]
    side = math.isqrt(snap)
    grid = Mesh(
        mesh.devices.reshape(snap // side, side, mesh.shape["mesh"]), ("r", "c", "mesh")
    )
    return jax.shard_map(
        local,
        mesh=grid,
        in_specs=(P("mesh", ("r", "c")), P("mesh", None), P()),
        out_specs=P(("r", "c"), "mesh"),
        check_vma=False,
    )
```

profile of v0, /device:TPU:31, one launch (start us, length us, event | category | flops | bytes accessed | tf_op | source)
XLA Modules:
  0.0 198.9 jit_solution(9688875784802368299)
XLA Ops:
  0.0 2.7 %fusion.23 = (f32[1536,128]{1,0:T(8,128)}, f32[1536,128]{1,0:T(8,128)}) fusion(f32[3072,128]{1,0:T(8,128)} %param.3), kind=kLoop, calls=%fused_computation.108 | loop fusion | bytes 3145728 | tf_op jit(solution)/shard_map/slice | solution.py:79
  2.7 6.0 %collective-permute-start.5 = (f32[1536,128]{1,0:T(8,128)}, f32[1536,128]{1,0:T(8,128)S(1)}, u32[]{:S(2)}, u32[]{:S(2)}) collective-permute-start(f32[1536,128]{1,0:T(8,128)} %get-tuple-element.10), channel_id=1, source_target_pairs={{0,192},{64,0},{128,64},{192,128},{1,193},{65,1},{129,65},{193,129... | collective-permute-start | bytes 2359304 | tf_op jit(solution)/shard_map/ppermute | solution.py:78
  9.9 2.4 %collective-permute-start.7 = (f32[1536,128]{1,0:T(8,128)}, f32[1536,128]{1,0:T(8,128)}, u32[]{:S(2)}, u32[]{:S(2)}) collective-permute-start(f32[1536,128]{1,0:T(8,128)} %get-tuple-element.11), channel_id=1, source_target_pairs={{0,192},{64,0},{128,64},{192,128},{1,193},{65,1},{129,65},{193,129... | collective-permute-start | bytes 2359304 | tf_op jit(solution)/shard_map/ppermute | solution.py:80
  13.1 3.4 %collective-permute-start = (f32[512,128]{1,0:T(8,128)}, f32[512,128]{1,0:T(8,128)S(1)}, u32[]{:S(2)}, u32[]{:S(2)}) collective-permute-start(f32[512,128]{1,0:T(8,128)} %slice.52), channel_id=1, source_target_pairs={{1,0},{2,1},{3,2},{4,3},{5,4},{6,5},{7,6},{8,7},{9,8},{10,9},{11,1... | collective-permute-start | bytes 786440 | tf_op jit(solution)/shard_map/ppermute | solution.py:16
  18.6 1.3 add_multiply_fusion.2
  19.9 1.3 collective-permute-start.1
  21.9 3.8 %collective-permute-done.1 = f32[512,128]{1,0:T(8,128)S(1)} collective-permute-done((f32[512,128]{1,0:T(8,128)S(1)}, f32[512,128]{1,0:T(8,128)S(1)}, u32[]{:S(2)}, u32[]{:S(2)}) %collective-permute-start.1) | collective-permute-done | bytes 262176 | tf_op jit(solution)/shard_map/ppermute | solution.py:16
  27.1 1.5 convolution_bitcast_fusion.15
  28.5 26.7 %collective-permute-done.2 = f32[1536,128]{1,0:T(8,128)S(1)} collective-permute-done((f32[1536,128]{1,0:T(8,128)}, f32[1536,128]{1,0:T(8,128)S(1)}, u32[]{:S(2)}, u32[]{:S(2)}) %collective-permute-start.2) | collective-permute-done | bytes 786464 | tf_op jit(solution)/shard_map/ppermute | solution.py:77
  55.2 25.9 %collective-permute-start.11 = (f32[1536,128]{1,0:T(8,128)S(1)}, f32[1536,128]{1,0:T(8,128)S(1)}, u32[]{:S(2)}, u32[]{:S(2)}) collective-permute-start(f32[1536,128]{1,0:T(8,128)S(1)} %bitcast.95), channel_id=1, source_target_pairs={{0,32},{16,48},{32,0},{48,16},{1,33},{17,49},{33,1},{49,17},{2,34}... | collective-permute-start | bytes 2359304 | tf_op jit(solution)/shard_map/ppermute | solution.py:66
  83.8 1.5 convolution_bitcast_fusion.12
  86.7 1.5 convolution_bitcast_fusion.14
  88.2 25.5 %collective-permute-done.11 = f32[1536,128]{1,0:T(8,128)S(1)} collective-permute-done((f32[1536,128]{1,0:T(8,128)S(1)}, f32[1536,128]{1,0:T(8,128)S(1)}, u32[]{:S(2)}, u32[]{:S(2)}) %collective-permute-start.11) | collective-permute-done | bytes 786464 | tf_op jit(solution)/shard_map/ppermute | solution.py:66
  115.2 1.5 convolution_bitcast_fusion.10
  116.7 1.5 convolution_bitcast_fusion.8
  118.2 12.4 %collective-permute-done.10 = f32[1536,128]{1,0:T(8,128)S(1)} collective-permute-done((f32[1536,128]{1,0:T(8,128)S(1)}, f32[1536,128]{1,0:T(8,128)S(1)}, u32[]{:S(2)}, u32[]{:S(2)}) %collective-permute-start.10) | collective-permute-done | bytes 786464 | tf_op jit(solution)/shard_map/ppermute | solution.py:68
  130.7 1.5 convolution_bitcast_fusion.11
  132.2 1.5 convolution_bitcast_fusion.6
  133.7 2.5 %collective-permute-start.12 = (f32[1536,128]{1,0:T(8,128)S(1)}, f32[1536,128]{1,0:T(8,128)S(1)}, u32[]{:S(2)}, u32[]{:S(2)}) collective-permute-start(f32[1536,128]{1,0:T(8,128)S(1)} %collective-permute-done.8), channel_id=1, source_target_pairs={{0,32},{16,48},{32,0},{48,16},{1,33},{17,49},{33,1},{49,17},{2,34}... | collective-permute-start | bytes 2359304 | tf_op jit(solution)/shard_map/ppermute | solution.py:69
  136.2 1.5 convolution_bitcast_fusion.4
  137.7 1.5 convolution_bitcast_fusion.7
  139.1 9.3 %collective-permute-done.4 = f32[1536,128]{1,0:T(8,128)S(1)} collective-permute-done((f32[1536,128]{1,0:T(8,128)S(1)}, f32[1536,128]{1,0:T(8,128)S(1)}, u32[]{:S(2)}, u32[]{:S(2)}) %collective-permute-start.4) | collective-permute-done | bytes 786464 | tf_op jit(solution)/shard_map/ppermute | solution.py:81
  148.5 1.5 convolution_bitcast_fusion.9
  150.0 1.5 convolution_bitcast_fusion.13
  151.5 1.5 convolution_bitcast_fusion.5
  153.0 14.5 %collective-permute-done.12 = f32[1536,128]{1,0:T(8,128)S(1)} collective-permute-done((f32[1536,128]{1,0:T(8,128)S(1)}, f32[1536,128]{1,0:T(8,128)S(1)}, u32[]{:S(2)}, u32[]{:S(2)}) %collective-permute-start.12) | collective-permute-done | bytes 786464 | tf_op jit(solution)/shard_map/ppermute | solution.py:69
  167.6 1.5 convolution_bitcast_fusion.2
  169.1 1.5 convolution_bitcast_fusion.1
  170.6 1.5 convolution_bitcast_fusion
  172.0 1.4 convolution_bitcast_fusion.3
  177.5 20.0 %shard_map.37 = f32[128,128]{1,0:T(8,128)} custom-call(f32[8,128,128]{2,1,0:T(8,128)} %add.325.part_ref), custom_call_target="tpu_custom_call" | custom-call | tf_op jit(solution)/shard_map/pallas_call | solution.py:164
  197.4 1.5 broadcast_multiply_fusion
  (56 shorter events, 15.8 us)
Async XLA Ops:
  0.0 12.4 %copy-start = (f32[3072,128]{1,0:T(8,128)S(1)}, f32[3072,128]{1,0:T(8,128)}, u32[]{:S(2)}) copy-start(f32[3072,128]{1,0:T(8,128)} %param.3) | copy-start | bytes 4718596
  0.0 16.5 %copy-start.1 = (s32[6,512]{1,0:T(8,128)S(1)}, s32[6,512]{1,0:T(8,128)}, u32[]{:S(2)}) copy-start(s32[6,512]{1,0:T(8,128)} %param.4) | copy-start | bytes 36868
  0.0 16.5 %copy-start.2 = (f32[8]{0:T(128)S(1)}, f32[8]{0:T(128)}, u32[]{:S(2)}) copy-start(f32[8]{0:T(128)} %param.5) | copy-start | bytes 100
  2.7 80.9 %collective-permute-start.5 = (f32[1536,128]{1,0:T(8,128)}, f32[1536,128]{1,0:T(8,128)S(1)}, u32[]{:S(2)}, u32[]{:S(2)}) collective-permute-start(f32[1536,128]{1,0:T(8,128)} %get-tuple-element.10), channel_id=1, source_target_pairs={{0,192},{64,0},{128,64},{192,128},{1,193},{65,1},{129,65},{193,129... | collective-permute-start | bytes 2359304 | tf_op jit(solution)/shard_map/ppermute | solution.py:78
  8.7 76.5 %collective-permute-start.3 = (f32[1536,128]{1,0:T(8,128)}, f32[1536,128]{1,0:T(8,128)}, u32[]{:S(2)}, u32[]{:S(2)}) collective-permute-start(f32[1536,128]{1,0:T(8,128)} %get-tuple-element.10), channel_id=1, source_target_pairs={{0,64},{64,128},{128,192},{192,0},{1,65},{65,129},{129,193},{193,1... | collective-permute-start | bytes 2359304 | tf_op jit(solution)/shard_map/ppermute | solution.py:79
  8.7 46.5 %collective-permute-start.2 = (f32[1536,128]{1,0:T(8,128)}, f32[1536,128]{1,0:T(8,128)S(1)}, u32[]{:S(2)}, u32[]{:S(2)}) collective-permute-start(f32[1536,128]{1,0:T(8,128)} %get-tuple-element.11), channel_id=1, source_target_pairs={{0,64},{64,128},{128,192},{192,0},{1,65},{65,129},{129,193},{193,1... | collective-permute-start | bytes 2359304 | tf_op jit(solution)/shard_map/ppermute | solution.py:77
  9.9 71.3 %collective-permute-start.7 = (f32[1536,128]{1,0:T(8,128)}, f32[1536,128]{1,0:T(8,128)}, u32[]{:S(2)}, u32[]{:S(2)}) collective-permute-start(f32[1536,128]{1,0:T(8,128)} %get-tuple-element.11), channel_id=1, source_target_pairs={{0,192},{64,0},{128,64},{192,128},{1,193},{65,1},{129,65},{193,129... | collective-permute-start | bytes 2359304 | tf_op jit(solution)/shard_map/ppermute | solution.py:80
  13.1 4.8 %collective-permute-start = (f32[512,128]{1,0:T(8,128)}, f32[512,128]{1,0:T(8,128)S(1)}, u32[]{:S(2)}, u32[]{:S(2)}) collective-permute-start(f32[512,128]{1,0:T(8,128)} %slice.52), channel_id=1, source_target_pairs={{1,0},{2,1},{3,2},{4,3},{5,4},{6,5},{7,6},{8,7},{9,8},{10,9},{11,1... | collective-permute-start | bytes 786440 | tf_op jit(solution)/shard_map/ppermute | solution.py:16
  19.9 5.8 %collective-permute-start.1 = (f32[512,128]{1,0:T(8,128)S(1)}, f32[512,128]{1,0:T(8,128)S(1)}, u32[]{:S(2)}, u32[]{:S(2)}) collective-permute-start(f32[512,128]{1,0:T(8,128)S(1)} %add_bitcast_fusion), channel_id=1, source_target_pairs={{0,1},{1,2},{2,3},{3,4},{4,5},{5,6},{6,7},{7,8},{8,9},{9,10},{10,1... | collective-permute-start | bytes 786440 | tf_op jit(solution)/shard_map/ppermute | solution.py:16
  25.7 89.4 %collective-permute-start.9 = (f32[1536,128]{1,0:T(8,128)S(1)}, f32[1536,128]{1,0:T(8,128)S(1)}, u32[]{:S(2)}, u32[]{:S(2)}) collective-permute-start(f32[1536,128]{1,0:T(8,128)S(1)} %bitcast.94), channel_id=1, source_target_pairs={{0,16},{16,0},{32,48},{48,32},{1,17},{17,1},{33,49},{49,33},{2,18}... | collective-permute-start | bytes 2359304 | tf_op jit(solution)/shard_map/ppermute | solution.py:67
  55.2 58.5 %collective-permute-start.11 = (f32[1536,128]{1,0:T(8,128)S(1)}, f32[1536,128]{1,0:T(8,128)S(1)}, u32[]{:S(2)}, u32[]{:S(2)}) collective-permute-start(f32[1536,128]{1,0:T(8,128)S(1)} %bitcast.95), channel_id=1, source_target_pairs={{0,32},{16,48},{32,0},{48,16},{1,33},{17,49},{33,1},{49,17},{2,34}... | collective-permute-start | bytes 2359304 | tf_op jit(solution)/shard_map/ppermute | solution.py:66
  81.2 32.8 %collective-permute-start.8 = (f32[1536,128]{1,0:T(8,128)S(1)}, f32[1536,128]{1,0:T(8,128)S(1)}, u32[]{:S(2)}, u32[]{:S(2)}) collective-permute-start(f32[1536,128]{1,0:T(8,128)S(1)} %bitcast.96), channel_id=1, source_target_pairs={{0,16},{16,0},{32,48},{48,32},{1,17},{17,1},{33,49},{49,33},{2,18}... | collective-permute-start | bytes 2359304 | tf_op jit(solution)/shard_map/ppermute | solution.py:65
  83.6 47.0 %collective-permute-start.10 = (f32[1536,128]{1,0:T(8,128)S(1)}, f32[1536,128]{1,0:T(8,128)S(1)}, u32[]{:S(2)}, u32[]{:S(2)}) collective-permute-start(f32[1536,128]{1,0:T(8,128)S(1)} %bitcast.97), channel_id=1, source_target_pairs={{0,32},{16,48},{32,0},{48,16},{1,33},{17,49},{33,1},{49,17},{2,34}... | collective-permute-start | bytes 2359304 | tf_op jit(solution)/shard_map/ppermute | solution.py:68
  85.3 63.1 %collective-permute-start.4 = (f32[1536,128]{1,0:T(8,128)S(1)}, f32[1536,128]{1,0:T(8,128)S(1)}, u32[]{:S(2)}, u32[]{:S(2)}) collective-permute-start(f32[1536,128]{1,0:T(8,128)S(1)} %collective-permute-done.2), channel_id=1, source_target_pairs={{0,64},{64,128},{128,192},{192,0},{1,65},{65,129},{129,193},{193,1... | collective-permute-start | bytes 2359304 | tf_op jit(solution)/shard_map/ppermute | solution.py:81
  113.7 34.7 %collective-permute-start.6 = (f32[1536,128]{1,0:T(8,128)S(1)}, f32[1536,128]{1,0:T(8,128)S(1)}, u32[]{:S(2)}, u32[]{:S(2)}) collective-permute-start(f32[1536,128]{1,0:T(8,128)S(1)} %collective-permute-done.5), channel_id=1, source_target_pairs={{0,192},{64,0},{128,64},{192,128},{1,193},{65,1},{129,65},{193,129... | collective-permute-start | bytes 2359304 | tf_op jit(solution)/shard_map/ppermute | solution.py:81
  113.9 53.6 %collective-permute-start.13 = (f32[1536,128]{1,0:T(8,128)S(1)}, f32[1536,128]{1,0:T(8,128)S(1)}, u32[]{:S(2)}, u32[]{:S(2)}) collective-permute-start(f32[1536,128]{1,0:T(8,128)S(1)} %collective-permute-done.11), channel_id=1, source_target_pairs={{0,16},{16,0},{32,48},{48,32},{1,17},{17,1},{33,49},{49,33},{2,18}... | collective-permute-start | bytes 2359304 | tf_op jit(solution)/shard_map/ppermute | solution.py:69
  133.7 33.8 %collective-permute-start.12 = (f32[1536,128]{1,0:T(8,128)S(1)}, f32[1536,128]{1,0:T(8,128)S(1)}, u32[]{:S(2)}, u32[]{:S(2)}) collective-permute-start(f32[1536,128]{1,0:T(8,128)S(1)} %collective-permute-done.8), channel_id=1, source_target_pairs={{0,32},{16,48},{32,0},{48,16},{1,33},{17,49},{33,1},{49,17},{2,34}... | collective-permute-start | bytes 2359304 | tf_op jit(solution)/shard_map/ppermute | solution.py:69
  174.2 2.4 %collective-permute-start.14 = (f32[8,128,128]{2,1,0:T(8,128)S(1)}, f32[8,128,128]{2,1,0:T(8,128)S(1)}, u32[]{:S(2)}, u32[]{:S(2)}) collective-permute-start(f32[8,128,128]{2,1,0:T(8,128)S(1)} %gather_fusion.1), channel_id=1, source_target_pairs={{0,1},{1,0},{2,3},{3,2},{4,5},{5,4},{6,7},{7,6},{8,9},{9,8},{10,11... | collective-permute-start | bytes 1572872 | tf_op jit(solution)/shard_map/ppermute | solution.py:163
where the time goes:
time: 202 us; the launch traced here: 199 us
  waiting for transfers between devices  94.3 us (47%)
  starting transfers between devices  47.7 us (24%)
  matrix products  23.6 us (12%)
  Pallas kernels  20 us (10%)
  local copies, waits for them, and re-layouts  7.59 us (4%)
  other arithmetic  5.47 us (3%)
    ppermute x1, waiting for transfers between devices, ring_gather(): left_low = lax.ppermute(block[:half], axis, up)  26.7 us
    ppermute x1, starting transfers between devices, square_gather(): z_high = lax.ppermute(block[half:], axis, to_z)  25.9 us
    ppermute x1, waiting for transfers between devices, square_gather(): z_high = lax.ppermute(block[half:], axis, to_z)  25.5 us
    dot_general x16, matrix products, contract(): lax.dot_general(left, right, (((0,), (0,)), ((), ())), precision=lax.Prec...  23.6 us
    pallas_call x1, Pallas kernels, scatter_to_owners(): pl.pallas_call(functools.partial(owners_kernel, side, tiles), out_shape=j...  20 us
    ppermute x2, waiting for transfers between devices, square_gather(): corner = [lax.ppermute(x_low, axis, to_z), lax.ppermute(z_high, axis, to_x)]  14.5 us
    ppermute x1, waiting for transfers between devices, square_gather(): z_low = lax.ppermute(block[:half], axis, to_z)  12.4 us
    ppermute x1, waiting for transfers between devices, ring_gather(): lax.ppermute(left_low, axis, up)  9.25 us
  transfers between devices with their start and end apart: 15, of which 8 were waited for; matrix products, arithmetic and copies ran while one was open for 13% of the time, Pallas kernels for 0%

commit v1 on v0

--- a/solution.py
+++ b/solution.py
@@ -191,8 +191,19 @@
     )
     rows = square_gather(panel, "c")
     cols = ring_gather(snapshots, "r")
+    relayed_row, relayed_col = len(rows) - 1, len(cols) // 2
+
+    def product(k1, k2):
+        if k1 == relayed_row or k2 == relayed_col:
+            half = node_rows // 2
+            a, b = rows[k1], cols[k2]
+            a = a if isinstance(a, list) else [a[:half], a[half:]]
+            b = b if isinstance(b, list) else [b[:half], b[half:]]
+            return contract(a[0], b[0]) + contract(a[1], b[1])
+        return contract(joined(rows[k1]), joined(cols[k2]))
+
     blocks = jnp.stack(
-        [jnp.stack([contract(joined(a), joined(b)) for b in cols], 0) for a in rows], 0
+        [jnp.stack([product(k1, k2) for k2 in range(side)], 0) for k1 in range(side)], 0
     )
     placed = scatter_to_owners(blocks, side, tiles)
     total_nodes = node_rows * tiles

time: 202 us -> 198 us (0.980)
  starting transfers between devices: 47.7 us -> 26.7 us
  waiting for transfers between devices: 94.3 us -> 105 us
  matrix products: 23.6 us -> 27.1 us
  Pallas kernels: 20 us -> 23 us
    ppermute x1, waiting for transfers between devices: 26.7 us -> 0.01 us  [ring_gather(): left_low = lax.ppermute(block[:half], axis, up)]
    ppermute x1, starting transfers between devices: 25.9 us -> 0.74 us  [square_gather(): z_high = lax.ppermute(block[half:], axis, to_z)]
    ppermute x1, waiting for transfers between devices: 0.01 us -> 23.7 us  [ring_gather(): right_low = lax.ppermute(block[:half], axis, down)]
    ppermute x1, waiting for transfers between devices: 0.01 us -> 19.7 us  [ring_gather(): right_high = lax.ppermute(block[half:], axis, down)]
    ppermute x2, waiting for transfers between devices: 14.5 us -> 6.36 us  [square_gather(): corner = [lax.ppermute(x_low, axis, to_z), lax.ppermute(z_high, axis, to_x)]]
    ppermute x1, waiting for transfers between devices: 12.4 us -> 16.8 us  [square_gather(): z_low = lax.ppermute(block[:half], axis, to_z)]
    ppermute x1, starting transfers between devices: 0.21 us -> 4.61 us  [ring_gather(): lax.ppermute(right_high, axis, down)]
    ppermute x1, starting transfers between devices: 2.43 us -> 6.02 us  [ring_gather(): right_low = lax.ppermute(block[:half], axis, down)]
  transfers between devices with their start and end apart: 15 -> 15, of which waited for: 8 -> 9; matrix products, arithmetic and copies ran while one was open for 13% -> 15% of each run, Pallas kernels for 0% -> 0%
where the time goes in v1:
time: 198 us; the launch traced here: 195 us
  waiting for transfers between devices  105 us (53%)
  matrix products  27.1 us (14%)
  starting transfers between devices  26.7 us (13%)
  Pallas kernels  23 us (12%)
  local copies, waits for them, and re-layouts  7.45 us (4%)
  other arithmetic  5.5 us (3%)
    dot_general x23, matrix products, contract(): lax.dot_general(left, right, (((0,), (0,)), ((), ())), precision=lax.Prec...  27.1 us
    ppermute x1, waiting for transfers between devices, square_gather(): z_high = lax.ppermute(block[half:], axis, to_z)  24.2 us
    ppermute x1, waiting for transfers between devices, ring_gather(): right_low = lax.ppermute(block[:half], axis, down)  23.7 us
    pallas_call x1, Pallas kernels, scatter_to_owners(): pl.pallas_call(functools.partial(owners_kernel, side, tiles), out_shape=j...  23 us
    ppermute x1, waiting for transfers between devices, ring_gather(): right_high = lax.ppermute(block[half:], axis, down)  19.7 us
    ppermute x1, waiting for transfers between devices, square_gather(): z_low = lax.ppermute(block[:half], axis, to_z)  16.8 us
    ppermute x1, waiting for transfers between devices, ring_gather(): lax.ppermute(left_low, axis, up)  8.36 us
    ppermute x2, waiting for transfers between devices, square_gather(): corner = [lax.ppermute(x_low, axis, to_z), lax.ppermute(z_high, axis, to_x)]  6.36 us
  transfers between devices with their start and end apart: 15, of which 9 were waited for; matrix products, arithmetic and copies ran while one was open for 15% of the time, Pallas kernels for 0%

profile of v1, /device:TPU:31, one launch (start us, length us, event | category | flops | bytes accessed | tf_op | source)
XLA Modules:
  0.0 195.3 jit_solution(3562589741786524794)
XLA Ops:
  0.0 2.8 %fusion.33 = (f32[1536,128]{1,0:T(8,128)}, f32[1536,128]{1,0:T(8,128)}) fusion(f32[3072,128]{1,0:T(8,128)} %param.3), kind=kLoop, calls=%fused_computation.114 | loop fusion | bytes 3145728 | tf_op jit(solution)/shard_map/slice | solution.py:77
  2.8 6.0 %collective-permute-start.7 = (f32[1536,128]{1,0:T(8,128)}, f32[1536,128]{1,0:T(8,128)}, u32[]{:S(2)}, u32[]{:S(2)}) collective-permute-start(f32[1536,128]{1,0:T(8,128)} %get-tuple-element.10), channel_id=1, source_target_pairs={{0,192},{64,0},{128,64},{192,128},{1,193},{65,1},{129,65},{193,129... | collective-permute-start | bytes 2359304 | tf_op jit(solution)/shard_map/ppermute | solution.py:80
  8.8 3.6 %collective-permute-start.5 = (f32[1536,128]{1,0:T(8,128)}, f32[1536,128]{1,0:T(8,128)S(1)}, u32[]{:S(2)}, u32[]{:S(2)}) collective-permute-start(f32[1536,128]{1,0:T(8,128)} %get-tuple-element.11), channel_id=1, source_target_pairs={{0,192},{64,0},{128,64},{192,128},{1,193},{65,1},{129,65},{193,129... | collective-permute-start | bytes 2359304 | tf_op jit(solution)/shard_map/ppermute | solution.py:78
  13.1 3.4 %collective-permute-start = (f32[512,128]{1,0:T(8,128)}, f32[512,128]{1,0:T(8,128)S(1)}, u32[]{:S(2)}, u32[]{:S(2)}) collective-permute-start(f32[512,128]{1,0:T(8,128)} %slice.56), channel_id=1, source_target_pairs={{1,0},{2,1},{3,2},{4,3},{5,4},{6,5},{7,6},{8,7},{9,8},{10,9},{11,1... | collective-permute-start | bytes 786440 | tf_op jit(solution)/shard_map/ppermute | solution.py:16
  18.7 1.3 add_multiply_fusion.2
  20.0 1.3 collective-permute-start.1
  21.9 3.8 %collective-permute-done.1 = f32[512,128]{1,0:T(8,128)S(1)} collective-permute-done((f32[512,128]{1,0:T(8,128)S(1)}, f32[512,128]{1,0:T(8,128)S(1)}, u32[]{:S(2)}, u32[]{:S(2)}) %collective-permute-start.1) | collective-permute-done | bytes 262176 | tf_op jit(solution)/shard_map/ppermute | solution.py:16
  26.6 1.5 convolution_bitcast_fusion.8
  28.2 23.7 %collective-permute-done.7 = f32[1536,128]{1,0:T(8,128)} collective-permute-done((f32[1536,128]{1,0:T(8,128)}, f32[1536,128]{1,0:T(8,128)}, u32[]{:S(2)}, u32[]{:S(2)}) %collective-permute-start.7) | collective-permute-done | bytes 786464 | tf_op jit(solution)/shard_map/ppermute | solution.py:80
  53.0 1.2 constant_dynamic-update-slice_fusion.3
  54.2 19.7 %collective-permute-done.5 = f32[1536,128]{1,0:T(8,128)S(1)} collective-permute-done((f32[1536,128]{1,0:T(8,128)}, f32[1536,128]{1,0:T(8,128)S(1)}, u32[]{:S(2)}, u32[]{:S(2)}) %collective-permute-start.5) | collective-permute-done | bytes 786464 | tf_op jit(solution)/shard_map/ppermute | solution.py:78
  73.9 2.0 %collective-permute-start.10 = (f32[1536,128]{1,0:T(8,128)S(1)}, f32[1536,128]{1,0:T(8,128)S(1)}, u32[]{:S(2)}, u32[]{:S(2)}) collective-permute-start(f32[1536,128]{1,0:T(8,128)S(1)} %bitcast.106), channel_id=1, source_target_pairs={{0,32},{16,48},{32,0},{48,16},{1,33},{17,49},{33,1},{49,17},{2,34}... | collective-permute-start | bytes 2359304 | tf_op jit(solution)/shard_map/ppermute | solution.py:68
  76.0 1.5 convolution_bitcast_fusion.6
  77.5 1.2 collective-permute-start.8
  78.7 1.2 constant_dynamic-update-slice_fusion.1
  79.9 4.6 %collective-permute-start.6 = (f32[1536,128]{1,0:T(8,128)S(1)}, f32[1536,128]{1,0:T(8,128)S(1)}, u32[]{:S(2)}, u32[]{:S(2)}) collective-permute-start(f32[1536,128]{1,0:T(8,128)S(1)} %collective-permute-done.5), channel_id=1, source_target_pairs={{0,192},{64,0},{128,64},{192,128},{1,193},{65,1},{129,65},{193,129... | collective-permute-start | bytes 2359304 | tf_op jit(solution)/shard_map/ppermute | solution.py:81
  84.6 1.5 convolution_bitcast_fusion.7
  86.0 24.2 %collective-permute-done.11 = f32[1536,128]{1,0:T(8,128)S(1)} collective-permute-done((f32[1536,128]{1,0:T(8,128)S(1)}, f32[1536,128]{1,0:T(8,128)S(1)}, u32[]{:S(2)}, u32[]{:S(2)}) %collective-permute-start.11) | collective-permute-done | bytes 786464 | tf_op jit(solution)/shard_map/ppermute | solution.py:66
  110.3 16.8 %collective-permute-done.10 = f32[1536,128]{1,0:T(8,128)S(1)} collective-permute-done((f32[1536,128]{1,0:T(8,128)S(1)}, f32[1536,128]{1,0:T(8,128)S(1)}, u32[]{:S(2)}, u32[]{:S(2)}) %collective-permute-start.10) | collective-permute-done | bytes 786464 | tf_op jit(solution)/shard_map/ppermute | solution.py:68
  128.4 1.5 convolution_bitcast_fusion
  129.8 1.5 convolution_bitcast_fusion.1
  131.5 1.5 convolution_bitcast_fusion.2
  132.9 1.5 convolution_bitcast_fusion.3
  134.4 1.5 convolution_bitcast_fusion.4
  136.2 1.5 convolution_bitcast_fusion.5
  139.4 8.4 %collective-permute-done.4 = f32[1536,128]{1,0:T(8,128)S(1)} collective-permute-done((f32[1536,128]{1,0:T(8,128)}, f32[1536,128]{1,0:T(8,128)S(1)}, u32[]{:S(2)}, u32[]{:S(2)}) %collective-permute-start.4) | collective-permute-done | bytes 786464 | tf_op jit(solution)/shard_map/ppermute | solution.py:81
  154.5 6.4 %collective-permute-done.12 = f32[1536,128]{1,0:T(8,128)S(1)} collective-permute-done((f32[1536,128]{1,0:T(8,128)S(1)}, f32[1536,128]{1,0:T(8,128)S(1)}, u32[]{:S(2)}, u32[]{:S(2)}) %collective-permute-start.12) | collective-permute-done | bytes 786464 | tf_op jit(solution)/shard_map/ppermute | solution.py:69
  160.8 2.0 fusion.1
  163.6 2.0 fusion.3
  167.1 1.2 collective-permute-start.14
  170.8 23.0 %shard_map.37 = f32[128,128]{1,0:T(8,128)} custom-call(f32[8,128,128]{2,1,0:T(8,128)} %add.353.part_ref), custom_call_target="tpu_custom_call" | custom-call | tf_op jit(solution)/shard_map/pallas_call | solution.py:164
  193.8 1.5 broadcast_multiply_fusion
  (61 shorter events, 20.3 us)
Async XLA Ops:
  0.0 12.4 %copy-start = (f32[3072,128]{1,0:T(8,128)S(1)}, f32[3072,128]{1,0:T(8,128)}, u32[]{:S(2)}) copy-start(f32[3072,128]{1,0:T(8,128)} %param.3) | copy-start | bytes 4718596
  0.0 16.6 %copy-start.2 = (f32[8]{0:T(128)S(1)}, f32[8]{0:T(128)}, u32[]{:S(2)}) copy-start(f32[8]{0:T(128)} %param.5) | copy-start | bytes 100
  0.0 16.6 %copy-start.1 = (s32[6,512]{1,0:T(8,128)S(1)}, s32[6,512]{1,0:T(8,128)}, u32[]{:S(2)}) copy-start(s32[6,512]{1,0:T(8,128)} %param.4) | copy-start | bytes 36868
  2.8 49.1 %collective-permute-start.7 = (f32[1536,128]{1,0:T(8,128)}, f32[1536,128]{1,0:T(8,128)}, u32[]{:S(2)}, u32[]{:S(2)}) collective-permute-start(f32[1536,128]{1,0:T(8,128)} %get-tuple-element.10), channel_id=1, source_target_pairs={{0,192},{64,0},{128,64},{192,128},{1,193},{65,1},{129,65},{193,129... | collective-permute-start | bytes 2359304 | tf_op jit(solution)/shard_map/ppermute | solution.py:80
  8.8 68.7 %collective-permute-start.2 = (f32[1536,128]{1,0:T(8,128)}, f32[1536,128]{1,0:T(8,128)}, u32[]{:S(2)}, u32[]{:S(2)}) collective-permute-start(f32[1536,128]{1,0:T(8,128)} %get-tuple-element.10), channel_id=1, source_target_pairs={{0,64},{64,128},{128,192},{192,0},{1,65},{65,129},{129,193},{193,1... | collective-permute-start | bytes 2359304 | tf_op jit(solution)/shard_map/ppermute | solution.py:77
  8.8 65.1 %collective-permute-start.5 = (f32[1536,128]{1,0:T(8,128)}, f32[1536,128]{1,0:T(8,128)S(1)}, u32[]{:S(2)}, u32[]{:S(2)}) collective-permute-start(f32[1536,128]{1,0:T(8,128)} %get-tuple-element.11), channel_id=1, source_target_pairs={{0,192},{64,0},{128,64},{192,128},{1,193},{65,1},{129,65},{193,129... | collective-permute-start | bytes 2359304 | tf_op jit(solution)/shard_map/ppermute | solution.py:78
  12.4 67.5 %collective-permute-start.3 = (f32[1536,128]{1,0:T(8,128)}, f32[1536,128]{1,0:T(8,128)S(1)}, u32[]{:S(2)}, u32[]{:S(2)}) collective-permute-start(f32[1536,128]{1,0:T(8,128)} %get-tuple-element.11), channel_id=1, source_target_pairs={{0,64},{64,128},{128,192},{192,0},{1,65},{65,129},{129,193},{193,1... | collective-permute-start | bytes 2359304 | tf_op jit(solution)/shard_map/ppermute | solution.py:79
  13.1 4.8 %collective-permute-start = (f32[512,128]{1,0:T(8,128)}, f32[512,128]{1,0:T(8,128)S(1)}, u32[]{:S(2)}, u32[]{:S(2)}) collective-permute-start(f32[512,128]{1,0:T(8,128)} %slice.56), channel_id=1, source_target_pairs={{1,0},{2,1},{3,2},{4,3},{5,4},{6,5},{7,6},{8,7},{9,8},{10,9},{11,1... | collective-permute-start | bytes 786440 | tf_op jit(solution)/shard_map/ppermute | solution.py:16
  20.0 5.8 %collective-permute-start.1 = (f32[512,128]{1,0:T(8,128)S(1)}, f32[512,128]{1,0:T(8,128)S(1)}, u32[]{:S(2)}, u32[]{:S(2)}) collective-permute-start(f32[512,128]{1,0:T(8,128)S(1)} %add_bitcast_fusion), channel_id=1, source_target_pairs={{0,1},{1,2},{2,3},{3,4},{4,5},{5,6},{6,7},{7,8},{8,9},{9,10},{10,1... | collective-permute-start | bytes 786440 | tf_op jit(solution)/shard_map/ppermute | solution.py:16
  25.7 84.5 %collective-permute-start.11 = (f32[1536,128]{1,0:T(8,128)S(1)}, f32[1536,128]{1,0:T(8,128)S(1)}, u32[]{:S(2)}, u32[]{:S(2)}) collective-permute-start(f32[1536,128]{1,0:T(8,128)S(1)} %bitcast.103), channel_id=1, source_target_pairs={{0,32},{16,48},{32,0},{48,16},{1,33},{17,49},{33,1},{49,17},{2,34}... | collective-permute-start | bytes 2359304 | tf_op jit(solution)/shard_map/ppermute | solution.py:66
  51.9 79.5 %collective-permute-start.9 = (f32[1536,128]{1,0:T(8,128)S(1)}, f32[1536,128]{1,0:T(8,128)S(1)}, u32[]{:S(2)}, u32[]{:S(2)}) collective-permute-start(f32[1536,128]{1,0:T(8,128)S(1)} %bitcast.104), channel_id=1, source_target_pairs={{0,16},{16,0},{32,48},{48,32},{1,17},{17,1},{33,49},{49,33},{2,18}... | collective-permute-start | bytes 2359304 | tf_op jit(solution)/shard_map/ppermute | solution.py:67
  73.9 53.2 %collective-permute-start.10 = (f32[1536,128]{1,0:T(8,128)S(1)}, f32[1536,128]{1,0:T(8,128)S(1)}, u32[]{:S(2)}, u32[]{:S(2)}) collective-permute-start(f32[1536,128]{1,0:T(8,128)S(1)} %bitcast.106), channel_id=1, source_target_pairs={{0,32},{16,48},{32,0},{48,16},{1,33},{17,49},{33,1},{49,17},{2,34}... | collective-permute-start | bytes 2359304 | tf_op jit(solution)/shard_map/ppermute | solution.py:68
  77.5 53.9 %collective-permute-start.8 = (f32[1536,128]{1,0:T(8,128)S(1)}, f32[1536,128]{1,0:T(8,128)S(1)}, u32[]{:S(2)}, u32[]{:S(2)}) collective-permute-start(f32[1536,128]{1,0:T(8,128)S(1)} %bitcast.107), channel_id=1, source_target_pairs={{0,16},{16,0},{32,48},{48,32},{1,17},{17,1},{33,49},{49,33},{2,18}... | collective-permute-start | bytes 2359304 | tf_op jit(solution)/shard_map/ppermute | solution.py:65
  79.9 57.8 %collective-permute-start.6 = (f32[1536,128]{1,0:T(8,128)S(1)}, f32[1536,128]{1,0:T(8,128)S(1)}, u32[]{:S(2)}, u32[]{:S(2)}) collective-permute-start(f32[1536,128]{1,0:T(8,128)S(1)} %collective-permute-done.5), channel_id=1, source_target_pairs={{0,192},{64,0},{128,64},{192,128},{1,193},{65,1},{129,65},{193,129... | collective-permute-start | bytes 2359304 | tf_op jit(solution)/shard_map/ppermute | solution.py:81
  110.3 37.5 %collective-permute-start.4 = (f32[1536,128]{1,0:T(8,128)}, f32[1536,128]{1,0:T(8,128)S(1)}, u32[]{:S(2)}, u32[]{:S(2)}) collective-permute-start(f32[1536,128]{1,0:T(8,128)} %collective-permute-done.2), channel_id=1, source_target_pairs={{0,64},{64,128},{128,192},{192,0},{1,65},{65,129},{129,193},{193,1... | collective-permute-start | bytes 2359304 | tf_op jit(solution)/shard_map/ppermute | solution.py:81
  127.1 24.0 %collective-permute-start.13 = (f32[1536,128]{1,0:T(8,128)S(1)}, f32[1536,128]{1,0:T(8,128)S(1)}, u32[]{:S(2)}, u32[]{:S(2)}) collective-permute-start(f32[1536,128]{1,0:T(8,128)S(1)} %collective-permute-done.11), channel_id=1, source_target_pairs={{0,16},{16,0},{32,48},{48,32},{1,17},{17,1},{33,49},{49,33},{2,18}... | collective-permute-start | bytes 2359304 | tf_op jit(solution)/shard_map/ppermute | solution.py:69
  135.9 24.9 %collective-permute-start.12 = (f32[1536,128]{1,0:T(8,128)S(1)}, f32[1536,128]{1,0:T(8,128)S(1)}, u32[]{:S(2)}, u32[]{:S(2)}) collective-permute-start(f32[1536,128]{1,0:T(8,128)S(1)} %collective-permute-done.8), channel_id=1, source_target_pairs={{0,32},{16,48},{32,0},{48,16},{1,33},{17,49},{33,1},{49,17},{2,34}... | collective-permute-start | bytes 2359304 | tf_op jit(solution)/shard_map/ppermute | solution.py:69
  167.1 2.8 %collective-permute-start.14 = (f32[8,128,128]{2,1,0:T(8,128)S(1)}, f32[8,128,128]{2,1,0:T(8,128)S(1)}, u32[]{:S(2)}, u32[]{:S(2)}) collective-permute-start(f32[8,128,128]{2,1,0:T(8,128)S(1)} %gather_fusion.1), channel_id=1, source_target_pairs={{0,1},{1,0},{2,3},{3,2},{4,5},{5,4},{6,7},{7,6},{8,9},{9,8},{10,11... | collective-permute-start | bytes 1572872 | tf_op jit(solution)/shard_map/ppermute | solution.py:163

commit v2 on v1

--- a/solution.py
+++ b/solution.py
@@ -95,6 +95,34 @@
     me_r, me_c, me_t = lax.axis_index("r"), lax.axis_index("c"), lax.axis_index("mesh")
     halves = tiles // 2
     parity = me_t % 2
+    incoming = (me_t // side) % 2
+
+    def same(a, b):
+        gap = a - b
+        return 1 - (gap * gap + 15) // 16
+
+    alone = same(me_t % side, me_c) * same(parity, incoming)
+    barrier = pltpu.get_barrier_semaphore()
+    for i in range(halves):
+        j = 2 * i + parity
+
+        @pl.when(jnp.logical_not(jnp.logical_and(j // side == me_c, me_c + side * (j % side) == me_t)))
+        def _():
+            pl.semaphore_signal(
+                barrier, 1, device_id=(me_r, j // side, me_c + side * (j % side)),
+                device_id_type=pl.DeviceIdType.MESH,
+            )
+
+    for source in range(halves):
+
+        @pl.when(jnp.logical_not(jnp.logical_and(alone == 1, me_t // 2 == source)))
+        def _():
+            pl.semaphore_signal(
+                barrier, 1, device_id=(me_r, me_t % side, 2 * source + incoming),
+                device_id_type=pl.DeviceIdType.MESH,
+            )
+
+    pl.semaphore_wait(barrier, 2 * (halves - alone))
     sends = []
     for i in range(halves):
         j = 2 * i + parity
@@ -121,8 +149,7 @@
         def _():
             slots[me_t // 2] = part_ref[i]
 
-    incoming = (me_t // side) % 2
-    mine = jnp.logical_and(me_t % side == me_c, parity == incoming)
+    mine = alone == 1
     for source in range(halves):
         arrival = pltpu.make_async_remote_copy(
             src_ref=slots.at[source],
@@ -171,7 +198,7 @@
             pltpu.SemaphoreType.DMA((halves,)),
             pltpu.SemaphoreType.DMA((halves,)),
         ],
-        compiler_params=pltpu.CompilerParams(has_side_effects=True),
+        compiler_params=pltpu.CompilerParams(collective_id=0, has_side_effects=True),
     )(kept)
 
 

time: 198 us -> 191 us (0.965)
  Pallas kernels: 23 us -> 15.7 us
    pallas_call x1, Pallas kernels: 23 us -> 15.7 us  [scatter_to_owners(): pl.pallas_call(functools.partial(owners_kernel, side, tiles), out_shape=j...]
where the time goes in v2:
time: 191 us; the launch traced here: 188 us
  waiting for transfers between devices  105 us (55%)
  matrix products  27.1 us (14%)
  starting transfers between devices  26.7 us (14%)
  Pallas kernels  15.7 us (8%)
  local copies, waits for them, and re-layouts  7.45 us (4%)
  other arithmetic  5.5 us (3%)
    dot_general x23, matrix products, contract(): lax.dot_general(left, right, (((0,), (0,)), ((), ())), precision=lax.Prec...  27.1 us
    ppermute x1, waiting for transfers between devices, square_gather(): z_high = lax.ppermute(block[half:], axis, to_z)  24.2 us
    ppermute x1, waiting for transfers between devices, ring_gather(): right_low = lax.ppermute(block[:half], axis, down)  23.7 us
    ppermute x1, waiting for transfers between devices, ring_gather(): right_high = lax.ppermute(block[half:], axis, down)  19.7 us
    ppermute x1, waiting for transfers between devices, square_gather(): z_low = lax.ppermute(block[:half], axis, to_z)  16.8 us
    pallas_call x1, Pallas kernels, scatter_to_owners(): pl.pallas_call(functools.partial(owners_kernel, side, tiles), out_shape=j...  15.7 us
    ppermute x1, waiting for transfers between devices, ring_gather(): lax.ppermute(left_low, axis, up)  8.36 us
    ppermute x2, waiting for transfers between devices, square_gather(): corner = [lax.ppermute(x_low, axis, to_z), lax.ppermute(z_high, axis, to_x)]  6.36 us
  transfers between devices with their start and end apart: 15, of which 9 were waited for; matrix products, arithmetic and copies ran while one was open for 15% of the time, Pallas kernels for 0%

profile of v2, /device:TPU:31, one launch (start us, length us, event | category | flops | bytes accessed | tf_op | source)
XLA Modules:
  0.0 188.0 jit_solution(14460576218312689392)
XLA Ops:
  0.0 2.8 %fusion.33 = (f32[1536,128]{1,0:T(8,128)}, f32[1536,128]{1,0:T(8,128)}) fusion(f32[3072,128]{1,0:T(8,128)} %param.3), kind=kLoop, calls=%fused_computation.114 | loop fusion | bytes 3145728 | tf_op jit(solution)/shard_map/slice | solution.py:77
  2.8 6.0 %collective-permute-start.7 = (f32[1536,128]{1,0:T(8,128)}, f32[1536,128]{1,0:T(8,128)}, u32[]{:S(2)}, u32[]{:S(2)}) collective-permute-start(f32[1536,128]{1,0:T(8,128)} %get-tuple-element.10), channel_id=1, source_target_pairs={{0,192},{64,0},{128,64},{192,128},{1,193},{65,1},{129,65},{193,129... | collective-permute-start | bytes 2359304 | tf_op jit(solution)/shard_map/ppermute | solution.py:80
  8.8 3.6 %collective-permute-start.5 = (f32[1536,128]{1,0:T(8,128)}, f32[1536,128]{1,0:T(8,128)S(1)}, u32[]{:S(2)}, u32[]{:S(2)}) collective-permute-start(f32[1536,128]{1,0:T(8,128)} %get-tuple-element.11), channel_id=1, source_target_pairs={{0,192},{64,0},{128,64},{192,128},{1,193},{65,1},{129,65},{193,129... | collective-permute-start | bytes 2359304 | tf_op jit(solution)/shard_map/ppermute | solution.py:78
  13.1 3.4 %collective-permute-start = (f32[512,128]{1,0:T(8,128)}, f32[512,128]{1,0:T(8,128)S(1)}, u32[]{:S(2)}, u32[]{:S(2)}) collective-permute-start(f32[512,128]{1,0:T(8,128)} %slice.56), channel_id=1, source_target_pairs={{1,0},{2,1},{3,2},{4,3},{5,4},{6,5},{7,6},{8,7},{9,8},{10,9},{11,1... | collective-permute-start | bytes 786440 | tf_op jit(solution)/shard_map/ppermute | solution.py:16
  18.7 1.3 add_multiply_fusion.2
  20.0 1.3 collective-permute-start.1
  21.9 3.8 %collective-permute-done.1 = f32[512,128]{1,0:T(8,128)S(1)} collective-permute-done((f32[512,128]{1,0:T(8,128)S(1)}, f32[512,128]{1,0:T(8,128)S(1)}, u32[]{:S(2)}, u32[]{:S(2)}) %collective-permute-start.1) | collective-permute-done | bytes 262176 | tf_op jit(solution)/shard_map/ppermute | solution.py:16
  26.6 1.5 convolution_bitcast_fusion.8
  28.2 23.7 %collective-permute-done.7 = f32[1536,128]{1,0:T(8,128)} collective-permute-done((f32[1536,128]{1,0:T(8,128)}, f32[1536,128]{1,0:T(8,128)}, u32[]{:S(2)}, u32[]{:S(2)}) %collective-permute-start.7) | collective-permute-done | bytes 786464 | tf_op jit(solution)/shard_map/ppermute | solution.py:80
  53.0 1.2 constant_dynamic-update-slice_fusion.3
  54.2 19.7 %collective-permute-done.5 = f32[1536,128]{1,0:T(8,128)S(1)} collective-permute-done((f32[1536,128]{1,0:T(8,128)}, f32[1536,128]{1,0:T(8,128)S(1)}, u32[]{:S(2)}, u32[]{:S(2)}) %collective-permute-start.5) | collective-permute-done | bytes 786464 | tf_op jit(solution)/shard_map/ppermute | solution.py:78
  73.9 2.0 %collective-permute-start.10 = (f32[1536,128]{1,0:T(8,128)S(1)}, f32[1536,128]{1,0:T(8,128)S(1)}, u32[]{:S(2)}, u32[]{:S(2)}) collective-permute-start(f32[1536,128]{1,0:T(8,128)S(1)} %bitcast.106), channel_id=1, source_target_pairs={{0,32},{16,48},{32,0},{48,16},{1,33},{17,49},{33,1},{49,17},{2,34}... | collective-permute-start | bytes 2359304 | tf_op jit(solution)/shard_map/ppermute | solution.py:68
  76.0 1.5 convolution_bitcast_fusion.6
  77.5 1.2 collective-permute-start.8
  78.7 1.2 constant_dynamic-update-slice_fusion.1
  79.9 4.6 %collective-permute-start.6 = (f32[1536,128]{1,0:T(8,128)S(1)}, f32[1536,128]{1,0:T(8,128)S(1)}, u32[]{:S(2)}, u32[]{:S(2)}) collective-permute-start(f32[1536,128]{1,0:T(8,128)S(1)} %collective-permute-done.5), channel_id=1, source_target_pairs={{0,192},{64,0},{128,64},{192,128},{1,193},{65,1},{129,65},{193,129... | collective-permute-start | bytes 2359304 | tf_op jit(solution)/shard_map/ppermute | solution.py:81
  84.6 1.5 convolution_bitcast_fusion.7
  86.0 24.2 %collective-permute-done.11 = f32[1536,128]{1,0:T(8,128)S(1)} collective-permute-done((f32[1536,128]{1,0:T(8,128)S(1)}, f32[1536,128]{1,0:T(8,128)S(1)}, u32[]{:S(2)}, u32[]{:S(2)}) %collective-permute-start.11) | collective-permute-done | bytes 786464 | tf_op jit(solution)/shard_map/ppermute | solution.py:66
  110.3 16.8 %collective-permute-done.10 = f32[1536,128]{1,0:T(8,128)S(1)} collective-permute-done((f32[1536,128]{1,0:T(8,128)S(1)}, f32[1536,128]{1,0:T(8,128)S(1)}, u32[]{:S(2)}, u32[]{:S(2)}) %collective-permute-start.10) | collective-permute-done | bytes 786464 | tf_op jit(solution)/shard_map/ppermute | solution.py:68
  128.4 1.5 convolution_bitcast_fusion
  129.8 1.5 convolution_bitcast_fusion.1
  131.5 1.5 convolution_bitcast_fusion.2
  132.9 1.5 convolution_bitcast_fusion.3
  134.4 1.5 convolution_bitcast_fusion.4
  136.2 1.5 convolution_bitcast_fusion.5
  139.4 8.4 %collective-permute-done.4 = f32[1536,128]{1,0:T(8,128)S(1)} collective-permute-done((f32[1536,128]{1,0:T(8,128)}, f32[1536,128]{1,0:T(8,128)S(1)}, u32[]{:S(2)}, u32[]{:S(2)}) %collective-permute-start.4) | collective-permute-done | bytes 786464 | tf_op jit(solution)/shard_map/ppermute | solution.py:81
  154.5 6.4 %collective-permute-done.12 = f32[1536,128]{1,0:T(8,128)S(1)} collective-permute-done((f32[1536,128]{1,0:T(8,128)S(1)}, f32[1536,128]{1,0:T(8,128)S(1)}, u32[]{:S(2)}, u32[]{:S(2)}) %collective-permute-start.12) | collective-permute-done | bytes 786464 | tf_op jit(solution)/shard_map/ppermute | solution.py:69
  160.8 2.0 %fusion.1 = f32[1,128,128]{2,1,0:T(8,128)S(1)} fusion(f32[128,128]{1,0:T(8,128)S(1)} %fusion.39, f32[1536,128]{1,0:T(8,128)S(1)} %collective-permute-done.12, f32[1536,128]{1,0:T(8,128)} %collective-permute-done.7), kind=kOutput, calls=%fused_computation.17 | convolution fusion | flops 151011328 | bytes 1703936 | tf_op jit(solution)/shard_map/dot_general | solution.py:49
  163.6 2.0 %fusion.3 = f32[1,128,128]{2,1,0:T(8,128)S(1)} fusion(f32[128,128]{1,0:T(8,128)S(1)} %fusion.37, f32[1536,128]{1,0:T(8,128)S(1)} %collective-permute-done.12, f32[1536,128]{1,0:T(8,128)} %collective-permute-done.2), kind=kOutput, calls=%fused_computation.21 | convolution fusion | flops 151011328 | bytes 1703936 | tf_op jit(solution)/shard_map/dot_general | solution.py:49
  167.1 1.2 collective-permute-start.14
  170.8 15.7 %shard_map.37 = f32[128,128]{1,0:T(8,128)} custom-call(f32[8,128,128]{2,1,0:T(8,128)} %add.353.part_ref), custom_call_target="tpu_custom_call" | custom-call | tf_op jit(solution)/shard_map/pallas_call | solution.py:191
  186.5 1.5 broadcast_multiply_fusion
  (61 shorter events, 20.3 us)
Async XLA Ops:
  0.0 12.4 %copy-start = (f32[3072,128]{1,0:T(8,128)S(1)}, f32[3072,128]{1,0:T(8,128)}, u32[]{:S(2)}) copy-start(f32[3072,128]{1,0:T(8,128)} %param.3) | copy-start | bytes 4718596
  0.0 16.6 %copy-start.2 = (f32[8]{0:T(128)S(1)}, f32[8]{0:T(128)}, u32[]{:S(2)}) copy-start(f32[8]{0:T(128)} %param.5) | copy-start | bytes 100
  0.0 16.6 %copy-start.1 = (s32[6,512]{1,0:T(8,128)S(1)}, s32[6,512]{1,0:T(8,128)}, u32[]{:S(2)}) copy-start(s32[6,512]{1,0:T(8,128)} %param.4) | copy-start | bytes 36868
  2.8 49.1 %collective-permute-start.7 = (f32[1536,128]{1,0:T(8,128)}, f32[1536,128]{1,0:T(8,128)}, u32[]{:S(2)}, u32[]{:S(2)}) collective-permute-start(f32[1536,128]{1,0:T(8,128)} %get-tuple-element.10), channel_id=1, source_target_pairs={{0,192},{64,0},{128,64},{192,128},{1,193},{65,1},{129,65},{193,129... | collective-permute-start | bytes 2359304 | tf_op jit(solution)/shard_map/ppermute | solution.py:80
  8.8 68.7 %collective-permute-start.2 = (f32[1536,128]{1,0:T(8,128)}, f32[1536,128]{1,0:T(8,128)}, u32[]{:S(2)}, u32[]{:S(2)}) collective-permute-start(f32[1536,128]{1,0:T(8,128)} %get-tuple-element.10), channel_id=1, source_target_pairs={{0,64},{64,128},{128,192},{192,0},{1,65},{65,129},{129,193},{193,1... | collective-permute-start | bytes 2359304 | tf_op jit(solution)/shard_map/ppermute | solution.py:77
  8.8 65.1 %collective-permute-start.5 = (f32[1536,128]{1,0:T(8,128)}, f32[1536,128]{1,0:T(8,128)S(1)}, u32[]{:S(2)}, u32[]{:S(2)}) collective-permute-start(f32[1536,128]{1,0:T(8,128)} %get-tuple-element.11), channel_id=1, source_target_pairs={{0,192},{64,0},{128,64},{192,128},{1,193},{65,1},{129,65},{193,129... | collective-permute-start | bytes 2359304 | tf_op jit(solution)/shard_map/ppermute | solution.py:78
  12.4 67.5 %collective-permute-start.3 = (f32[1536,128]{1,0:T(8,128)}, f32[1536,128]{1,0:T(8,128)S(1)}, u32[]{:S(2)}, u32[]{:S(2)}) collective-permute-start(f32[1536,128]{1,0:T(8,128)} %get-tuple-element.11), channel_id=1, source_target_pairs={{0,64},{64,128},{128,192},{192,0},{1,65},{65,129},{129,193},{193,1... | collective-permute-start | bytes 2359304 | tf_op jit(solution)/shard_map/ppermute | solution.py:79
  13.1 4.8 %collective-permute-start = (f32[512,128]{1,0:T(8,128)}, f32[512,128]{1,0:T(8,128)S(1)}, u32[]{:S(2)}, u32[]{:S(2)}) collective-permute-start(f32[512,128]{1,0:T(8,128)} %slice.56), channel_id=1, source_target_pairs={{1,0},{2,1},{3,2},{4,3},{5,4},{6,5},{7,6},{8,7},{9,8},{10,9},{11,1... | collective-permute-start | bytes 786440 | tf_op jit(solution)/shard_map/ppermute | solution.py:16
  20.0 5.8 %collective-permute-start.1 = (f32[512,128]{1,0:T(8,128)S(1)}, f32[512,128]{1,0:T(8,128)S(1)}, u32[]{:S(2)}, u32[]{:S(2)}) collective-permute-start(f32[512,128]{1,0:T(8,128)S(1)} %add_bitcast_fusion), channel_id=1, source_target_pairs={{0,1},{1,2},{2,3},{3,4},{4,5},{5,6},{6,7},{7,8},{8,9},{9,10},{10,1... | collective-permute-start | bytes 786440 | tf_op jit(solution)/shard_map/ppermute | solution.py:16
  25.7 84.5 %collective-permute-start.11 = (f32[1536,128]{1,0:T(8,128)S(1)}, f32[1536,128]{1,0:T(8,128)S(1)}, u32[]{:S(2)}, u32[]{:S(2)}) collective-permute-start(f32[1536,128]{1,0:T(8,128)S(1)} %bitcast.103), channel_id=1, source_target_pairs={{0,32},{16,48},{32,0},{48,16},{1,33},{17,49},{33,1},{49,17},{2,34}... | collective-permute-start | bytes 2359304 | tf_op jit(solution)/shard_map/ppermute | solution.py:66
  51.9 79.5 %collective-permute-start.9 = (f32[1536,128]{1,0:T(8,128)S(1)}, f32[1536,128]{1,0:T(8,128)S(1)}, u32[]{:S(2)}, u32[]{:S(2)}) collective-permute-start(f32[1536,128]{1,0:T(8,128)S(1)} %bitcast.104), channel_id=1, source_target_pairs={{0,16},{16,0},{32,48},{48,32},{1,17},{17,1},{33,49},{49,33},{2,18}... | collective-permute-start | bytes 2359304 | tf_op jit(solution)/shard_map/ppermute | solution.py:67
  73.9 53.2 %collective-permute-start.10 = (f32[1536,128]{1,0:T(8,128)S(1)}, f32[1536,128]{1,0:T(8,128)S(1)}, u32[]{:S(2)}, u32[]{:S(2)}) collective-permute-start(f32[1536,128]{1,0:T(8,128)S(1)} %bitcast.106), channel_id=1, source_target_pairs={{0,32},{16,48},{32,0},{48,16},{1,33},{17,49},{33,1},{49,17},{2,34}... | collective-permute-start | bytes 2359304 | tf_op jit(solution)/shard_map/ppermute | solution.py:68
  77.5 53.9 %collective-permute-start.8 = (f32[1536,128]{1,0:T(8,128)S(1)}, f32[1536,128]{1,0:T(8,128)S(1)}, u32[]{:S(2)}, u32[]{:S(2)}) collective-permute-start(f32[1536,128]{1,0:T(8,128)S(1)} %bitcast.107), channel_id=1, source_target_pairs={{0,16},{16,0},{32,48},{48,32},{1,17},{17,1},{33,49},{49,33},{2,18}... | collective-permute-start | bytes 2359304 | tf_op jit(solution)/shard_map/ppermute | solution.py:65
  79.9 57.8 %collective-permute-start.6 = (f32[1536,128]{1,0:T(8,128)S(1)}, f32[1536,128]{1,0:T(8,128)S(1)}, u32[]{:S(2)}, u32[]{:S(2)}) collective-permute-start(f32[1536,128]{1,0:T(8,128)S(1)} %collective-permute-done.5), channel_id=1, source_target_pairs={{0,192},{64,0},{128,64},{192,128},{1,193},{65,1},{129,65},{193,129... | collective-permute-start | bytes 2359304 | tf_op jit(solution)/shard_map/ppermute | solution.py:81
  110.3 37.5 %collective-permute-start.4 = (f32[1536,128]{1,0:T(8,128)}, f32[1536,128]{1,0:T(8,128)S(1)}, u32[]{:S(2)}, u32[]{:S(2)}) collective-permute-start(f32[1536,128]{1,0:T(8,128)} %collective-permute-done.2), channel_id=1, source_target_pairs={{0,64},{64,128},{128,192},{192,0},{1,65},{65,129},{129,193},{193,1... | collective-permute-start | bytes 2359304 | tf_op jit(solution)/shard_map/ppermute | solution.py:81
  127.1 24.0 %collective-permute-start.13 = (f32[1536,128]{1,0:T(8,128)S(1)}, f32[1536,128]{1,0:T(8,128)S(1)}, u32[]{:S(2)}, u32[]{:S(2)}) collective-permute-start(f32[1536,128]{1,0:T(8,128)S(1)} %collective-permute-done.11), channel_id=1, source_target_pairs={{0,16},{16,0},{32,48},{48,32},{1,17},{17,1},{33,49},{49,33},{2,18}... | collective-permute-start | bytes 2359304 | tf_op jit(solution)/shard_map/ppermute | solution.py:69
  135.9 24.9 %collective-permute-start.12 = (f32[1536,128]{1,0:T(8,128)S(1)}, f32[1536,128]{1,0:T(8,128)S(1)}, u32[]{:S(2)}, u32[]{:S(2)}) collective-permute-start(f32[1536,128]{1,0:T(8,128)S(1)} %collective-permute-done.8), channel_id=1, source_target_pairs={{0,32},{16,48},{32,0},{48,16},{1,33},{17,49},{33,1},{49,17},{2,34}... | collective-permute-start | bytes 2359304 | tf_op jit(solution)/shard_map/ppermute | solution.py:69
  167.1 2.8 %collective-permute-start.14 = (f32[8,128,128]{2,1,0:T(8,128)S(1)}, f32[8,128,128]{2,1,0:T(8,128)S(1)}, u32[]{:S(2)}, u32[]{:S(2)}) collective-permute-start(f32[8,128,128]{2,1,0:T(8,128)S(1)} %gather_fusion.1), channel_id=1, source_target_pairs={{0,1},{1,0},{2,3},{3,2},{4,5},{5,4},{6,7},{7,6},{8,9},{9,8},{10,11... | collective-permute-start | bytes 1572872 | tf_op jit(solution)/shard_map/ppermute | solution.py:190

commit v3 on v2

--- a/solution.py
+++ b/solution.py
@@ -176,7 +176,7 @@
     out_ref[...] = acc
 
 
-def scatter_to_owners(blocks, side, tiles):
+def scatter_to_owners(blocks, side, tiles, scale):
     width = blocks.shape[-1]
     me_r, me_c, me_t = lax.axis_index("r"), lax.axis_index("c"), lax.axis_index("mesh")
     halves = tiles // 2
@@ -187,7 +187,7 @@
         return blocks[two_bit_xor(me_c, j // side), (me_r - j % side) % side]
 
     parity = me_t % 2
-    kept = pieces(parity) + lax.ppermute(pieces(1 - parity), "mesh", pairs(tiles, lambda i: i ^ 1))
+    kept = (pieces(parity) + lax.ppermute(pieces(1 - parity), "mesh", pairs(tiles, lambda i: i ^ 1))) / scale
     return pl.pallas_call(
         functools.partial(owners_kernel, side, tiles),
         out_shape=jax.ShapeDtypeStruct((width, width), jnp.float32),
@@ -232,9 +232,7 @@
     blocks = jnp.stack(
         [jnp.stack([product(k1, k2) for k2 in range(side)], 0) for k1 in range(side)], 0
     )
-    placed = scatter_to_owners(blocks, side, tiles)
-    total_nodes = node_rows * tiles
-    return placed / math.sqrt(total_nodes)
+    return scatter_to_owners(blocks, side, tiles, math.sqrt(node_rows * tiles))
 
 
 def solution(mesh):

time: 191 us -> 191 us (level)
    unnamed x10 -> x11, local copies, waits for them, and re-layouts: 2.48 us -> 3.96 us
where the time goes in v3:
time: 191 us; the launch traced here: 188 us
  waiting for transfers between devices  105 us (55%)
  matrix products  27.1 us (14%)
  starting transfers between devices  26.7 us (14%)
  Pallas kernels  15.7 us (8%)
  local copies, waits for them, and re-layouts  8.92 us (5%)
  other arithmetic  4.03 us (2%)
    dot_general x23, matrix products, contract(): lax.dot_general(left, right, (((0,), (0,)), ((), ())), precision=lax.Prec...  27.1 us
    ppermute x1, waiting for transfers between devices, square_gather(): z_high = lax.ppermute(block[half:], axis, to_z)  24.2 us
    ppermute x1, waiting for transfers between devices, ring_gather(): right_low = lax.ppermute(block[:half], axis, down)  23.7 us
    ppermute x1, waiting for transfers between devices, ring_gather(): right_high = lax.ppermute(block[half:], axis, down)  19.7 us
    ppermute x1, waiting for transfers between devices, square_gather(): z_low = lax.ppermute(block[:half], axis, to_z)  16.8 us
    pallas_call x1, Pallas kernels, scatter_to_owners(): pl.pallas_call(functools.partial(owners_kernel, side, tiles), out_shape=j...  15.7 us
    ppermute x1, waiting for transfers between devices, ring_gather(): lax.ppermute(left_low, axis, up)  8.36 us
    ppermute x2, waiting for transfers between devices, square_gather(): corner = [lax.ppermute(x_low, axis, to_z), lax.ppermute(z_high, axis, to_x)]  6.36 us
  transfers between devices with their start and end apart: 15, of which 9 were waited for; matrix products, arithmetic and copies ran while one was open for 15% of the time, Pallas kernels for 0%

profile of v3, /device:TPU:31, one launch (start us, length us, event | category | flops | bytes accessed | tf_op | source)
XLA Modules:
  0.0 188.0 jit_solution(6018085866008869171)
XLA Ops:
  0.0 2.8 %fusion.33 = (f32[1536,128]{1,0:T(8,128)}, f32[1536,128]{1,0:T(8,128)}) fusion(f32[3072,128]{1,0:T(8,128)} %param.3), kind=kLoop, calls=%fused_computation.114 | loop fusion | bytes 3145728 | tf_op jit(solution)/shard_map/slice | solution.py:77
  2.8 6.0 %collective-permute-start.7 = (f32[1536,128]{1,0:T(8,128)}, f32[1536,128]{1,0:T(8,128)}, u32[]{:S(2)}, u32[]{:S(2)}) collective-permute-start(f32[1536,128]{1,0:T(8,128)} %get-tuple-element.10), channel_id=1, source_target_pairs={{0,192},{64,0},{128,64},{192,128},{1,193},{65,1},{129,65},{193,129... | collective-permute-start | bytes 2359304 | tf_op jit(solution)/shard_map/ppermute | solution.py:80
  8.8 3.6 %collective-permute-start.5 = (f32[1536,128]{1,0:T(8,128)}, f32[1536,128]{1,0:T(8,128)S(1)}, u32[]{:S(2)}, u32[]{:S(2)}) collective-permute-start(f32[1536,128]{1,0:T(8,128)} %get-tuple-element.11), channel_id=1, source_target_pairs={{0,192},{64,0},{128,64},{192,128},{1,193},{65,1},{129,65},{193,129... | collective-permute-start | bytes 2359304 | tf_op jit(solution)/shard_map/ppermute | solution.py:78
  13.1 3.4 %collective-permute-start = (f32[512,128]{1,0:T(8,128)}, f32[512,128]{1,0:T(8,128)S(1)}, u32[]{:S(2)}, u32[]{:S(2)}) collective-permute-start(f32[512,128]{1,0:T(8,128)} %slice.56), channel_id=1, source_target_pairs={{1,0},{2,1},{3,2},{4,3},{5,4},{6,5},{7,6},{8,7},{9,8},{10,9},{11,1... | collective-permute-start | bytes 786440 | tf_op jit(solution)/shard_map/ppermute | solution.py:16
  18.7 1.3 add_multiply_fusion.2
  20.0 1.3 collective-permute-start.1
  21.9 3.8 %collective-permute-done.1 = f32[512,128]{1,0:T(8,128)S(1)} collective-permute-done((f32[512,128]{1,0:T(8,128)S(1)}, f32[512,128]{1,0:T(8,128)S(1)}, u32[]{:S(2)}, u32[]{:S(2)}) %collective-permute-start.1) | collective-permute-done | bytes 262176 | tf_op jit(solution)/shard_map/ppermute | solution.py:16
  26.6 1.5 convolution_bitcast_fusion.8
  28.2 23.7 %collective-permute-done.7 = f32[1536,128]{1,0:T(8,128)} collective-permute-done((f32[1536,128]{1,0:T(8,128)}, f32[1536,128]{1,0:T(8,128)}, u32[]{:S(2)}, u32[]{:S(2)}) %collective-permute-start.7) | collective-permute-done | bytes 786464 | tf_op jit(solution)/shard_map/ppermute | solution.py:80
  53.0 1.2 constant_dynamic-update-slice_fusion.3
  54.2 19.7 %collective-permute-done.5 = f32[1536,128]{1,0:T(8,128)S(1)} collective-permute-done((f32[1536,128]{1,0:T(8,128)}, f32[1536,128]{1,0:T(8,128)S(1)}, u32[]{:S(2)}, u32[]{:S(2)}) %collective-permute-start.5) | collective-permute-done | bytes 786464 | tf_op jit(solution)/shard_map/ppermute | solution.py:78
  73.9 2.0 %collective-permute-start.10 = (f32[1536,128]{1,0:T(8,128)S(1)}, f32[1536,128]{1,0:T(8,128)S(1)}, u32[]{:S(2)}, u32[]{:S(2)}) collective-permute-start(f32[1536,128]{1,0:T(8,128)S(1)} %bitcast.106), channel_id=1, source_target_pairs={{0,32},{16,48},{32,0},{48,16},{1,33},{17,49},{33,1},{49,17},{2,34}... | collective-permute-start | bytes 2359304 | tf_op jit(solution)/shard_map/ppermute | solution.py:68
  76.0 1.5 convolution_bitcast_fusion.6
  77.5 1.2 collective-permute-start.8
  78.7 1.2 constant_dynamic-update-slice_fusion.1
  79.9 4.6 %collective-permute-start.6 = (f32[1536,128]{1,0:T(8,128)S(1)}, f32[1536,128]{1,0:T(8,128)S(1)}, u32[]{:S(2)}, u32[]{:S(2)}) collective-permute-start(f32[1536,128]{1,0:T(8,128)S(1)} %collective-permute-done.5), channel_id=1, source_target_pairs={{0,192},{64,0},{128,64},{192,128},{1,193},{65,1},{129,65},{193,129... | collective-permute-start | bytes 2359304 | tf_op jit(solution)/shard_map/ppermute | solution.py:81
  84.6 1.5 convolution_bitcast_fusion.7
  86.0 24.2 %collective-permute-done.11 = f32[1536,128]{1,0:T(8,128)S(1)} collective-permute-done((f32[1536,128]{1,0:T(8,128)S(1)}, f32[1536,128]{1,0:T(8,128)S(1)}, u32[]{:S(2)}, u32[]{:S(2)}) %collective-permute-start.11) | collective-permute-done | bytes 786464 | tf_op jit(solution)/shard_map/ppermute | solution.py:66
  110.3 16.8 %collective-permute-done.10 = f32[1536,128]{1,0:T(8,128)S(1)} collective-permute-done((f32[1536,128]{1,0:T(8,128)S(1)}, f32[1536,128]{1,0:T(8,128)S(1)}, u32[]{:S(2)}, u32[]{:S(2)}) %collective-permute-start.10) | collective-permute-done | bytes 786464 | tf_op jit(solution)/shard_map/ppermute | solution.py:68
  128.4 1.5 convolution_bitcast_fusion
  129.8 1.5 convolution_bitcast_fusion.1
  131.5 1.5 convolution_bitcast_fusion.2
  132.9 1.5 convolution_bitcast_fusion.3
  134.4 1.5 convolution_bitcast_fusion.4
  136.2 1.5 convolution_bitcast_fusion.5
  139.4 8.4 %collective-permute-done.4 = f32[1536,128]{1,0:T(8,128)S(1)} collective-permute-done((f32[1536,128]{1,0:T(8,128)}, f32[1536,128]{1,0:T(8,128)S(1)}, u32[]{:S(2)}, u32[]{:S(2)}) %collective-permute-start.4) | collective-permute-done | bytes 786464 | tf_op jit(solution)/shard_map/ppermute | solution.py:81
  154.5 6.4 %collective-permute-done.12 = f32[1536,128]{1,0:T(8,128)S(1)} collective-permute-done((f32[1536,128]{1,0:T(8,128)S(1)}, f32[1536,128]{1,0:T(8,128)S(1)}, u32[]{:S(2)}, u32[]{:S(2)}) %collective-permute-start.12) | collective-permute-done | bytes 786464 | tf_op jit(solution)/shard_map/ppermute | solution.py:69
  160.8 2.0 %fusion.1 = f32[1,128,128]{2,1,0:T(8,128)S(1)} fusion(f32[128,128]{1,0:T(8,128)S(1)} %fusion.39, f32[1536,128]{1,0:T(8,128)S(1)} %collective-permute-done.12, f32[1536,128]{1,0:T(8,128)} %collective-permute-done.7), kind=kOutput, calls=%fused_computation.17 | convolution fusion | flops 151011328 | bytes 1703936 | tf_op jit(solution)/shard_map/dot_general | solution.py:49
  163.6 2.0 %fusion.3 = f32[1,128,128]{2,1,0:T(8,128)S(1)} fusion(f32[128,128]{1,0:T(8,128)S(1)} %fusion.37, f32[1536,128]{1,0:T(8,128)S(1)} %collective-permute-done.12, f32[1536,128]{1,0:T(8,128)} %collective-permute-done.2), kind=kOutput, calls=%fused_computation.21 | convolution fusion | flops 151011328 | bytes 1703936 | tf_op jit(solution)/shard_map/dot_general | solution.py:49
  167.1 1.2 collective-permute-start.14
  170.8 15.7 %shard_map.37 = f32[128,128]{1,0:T(8,128)} custom-call(f32[8,128,128]{2,1,0:T(8,128)} %add_multiply_fusion.4.part_ref), custom_call_target="tpu_custom_call" | custom-call | tf_op jit(solution)/shard_map/pallas_call | solution.py:191
  186.5 1.5 copy.9
  (61 shorter events, 20.4 us)
Async XLA Ops:
  0.0 12.4 %copy-start = (f32[3072,128]{1,0:T(8,128)S(1)}, f32[3072,128]{1,0:T(8,128)}, u32[]{:S(2)}) copy-start(f32[3072,128]{1,0:T(8,128)} %param.3) | copy-start | bytes 4718596
  0.0 16.6 %copy-start.2 = (f32[8]{0:T(128)S(1)}, f32[8]{0:T(128)}, u32[]{:S(2)}) copy-start(f32[8]{0:T(128)} %param.5) | copy-start | bytes 100
  0.0 16.6 %copy-start.1 = (s32[6,512]{1,0:T(8,128)S(1)}, s32[6,512]{1,0:T(8,128)}, u32[]{:S(2)}) copy-start(s32[6,512]{1,0:T(8,128)} %param.4) | copy-start | bytes 36868
  2.8 49.1 %collective-permute-start.7 = (f32[1536,128]{1,0:T(8,128)}, f32[1536,128]{1,0:T(8,128)}, u32[]{:S(2)}, u32[]{:S(2)}) collective-permute-start(f32[1536,128]{1,0:T(8,128)} %get-tuple-element.10), channel_id=1, source_target_pairs={{0,192},{64,0},{128,64},{192,128},{1,193},{65,1},{129,65},{193,129... | collective-permute-start | bytes 2359304 | tf_op jit(solution)/shard_map/ppermute | solution.py:80
  8.8 68.7 %collective-permute-start.2 = (f32[1536,128]{1,0:T(8,128)}, f32[1536,128]{1,0:T(8,128)}, u32[]{:S(2)}, u32[]{:S(2)}) collective-permute-start(f32[1536,128]{1,0:T(8,128)} %get-tuple-element.10), channel_id=1, source_target_pairs={{0,64},{64,128},{128,192},{192,0},{1,65},{65,129},{129,193},{193,1... | collective-permute-start | bytes 2359304 | tf_op jit(solution)/shard_map/ppermute | solution.py:77
  8.8 65.1 %collective-permute-start.5 = (f32[1536,128]{1,0:T(8,128)}, f32[1536,128]{1,0:T(8,128)S(1)}, u32[]{:S(2)}, u32[]{:S(2)}) collective-permute-start(f32[1536,128]{1,0:T(8,128)} %get-tuple-element.11), channel_id=1, source_target_pairs={{0,192},{64,0},{128,64},{192,128},{1,193},{65,1},{129,65},{193,129... | collective-permute-start | bytes 2359304 | tf_op jit(solution)/shard_map/ppermute | solution.py:78
  12.4 67.5 %collective-permute-start.3 = (f32[1536,128]{1,0:T(8,128)}, f32[1536,128]{1,0:T(8,128)S(1)}, u32[]{:S(2)}, u32[]{:S(2)}) collective-permute-start(f32[1536,128]{1,0:T(8,128)} %get-tuple-element.11), channel_id=1, source_target_pairs={{0,64},{64,128},{128,192},{192,0},{1,65},{65,129},{129,193},{193,1... | collective-permute-start | bytes 2359304 | tf_op jit(solution)/shard_map/ppermute | solution.py:79
  13.1 4.8 %collective-permute-start = (f32[512,128]{1,0:T(8,128)}, f32[512,128]{1,0:T(8,128)S(1)}, u32[]{:S(2)}, u32[]{:S(2)}) collective-permute-start(f32[512,128]{1,0:T(8,128)} %slice.56), channel_id=1, source_target_pairs={{1,0},{2,1},{3,2},{4,3},{5,4},{6,5},{7,6},{8,7},{9,8},{10,9},{11,1... | collective-permute-start | bytes 786440 | tf_op jit(solution)/shard_map/ppermute | solution.py:16
  20.0 5.8 %collective-permute-start.1 = (f32[512,128]{1,0:T(8,128)S(1)}, f32[512,128]{1,0:T(8,128)S(1)}, u32[]{:S(2)}, u32[]{:S(2)}) collective-permute-start(f32[512,128]{1,0:T(8,128)S(1)} %add_bitcast_fusion), channel_id=1, source_target_pairs={{0,1},{1,2},{2,3},{3,4},{4,5},{5,6},{6,7},{7,8},{8,9},{9,10},{10,1... | collective-permute-start | bytes 786440 | tf_op jit(solution)/shard_map/ppermute | solution.py:16
  25.7 84.5 %collective-permute-start.11 = (f32[1536,128]{1,0:T(8,128)S(1)}, f32[1536,128]{1,0:T(8,128)S(1)}, u32[]{:S(2)}, u32[]{:S(2)}) collective-permute-start(f32[1536,128]{1,0:T(8,128)S(1)} %bitcast.103), channel_id=1, source_target_pairs={{0,32},{16,48},{32,0},{48,16},{1,33},{17,49},{33,1},{49,17},{2,34}... | collective-permute-start | bytes 2359304 | tf_op jit(solution)/shard_map/ppermute | solution.py:66
  51.9 79.5 %collective-permute-start.9 = (f32[1536,128]{1,0:T(8,128)S(1)}, f32[1536,128]{1,0:T(8,128)S(1)}, u32[]{:S(2)}, u32[]{:S(2)}) collective-permute-start(f32[1536,128]{1,0:T(8,128)S(1)} %bitcast.104), channel_id=1, source_target_pairs={{0,16},{16,0},{32,48},{48,32},{1,17},{17,1},{33,49},{49,33},{2,18}... | collective-permute-start | bytes 2359304 | tf_op jit(solution)/shard_map/ppermute | solution.py:67
  73.9 53.2 %collective-permute-start.10 = (f32[1536,128]{1,0:T(8,128)S(1)}, f32[1536,128]{1,0:T(8,128)S(1)}, u32[]{:S(2)}, u32[]{:S(2)}) collective-permute-start(f32[1536,128]{1,0:T(8,128)S(1)} %bitcast.106), channel_id=1, source_target_pairs={{0,32},{16,48},{32,0},{48,16},{1,33},{17,49},{33,1},{49,17},{2,34}... | collective-permute-start | bytes 2359304 | tf_op jit(solution)/shard_map/ppermute | solution.py:68
  77.5 53.9 %collective-permute-start.8 = (f32[1536,128]{1,0:T(8,128)S(1)}, f32[1536,128]{1,0:T(8,128)S(1)}, u32[]{:S(2)}, u32[]{:S(2)}) collective-permute-start(f32[1536,128]{1,0:T(8,128)S(1)} %bitcast.107), channel_id=1, source_target_pairs={{0,16},{16,0},{32,48},{48,32},{1,17},{17,1},{33,49},{49,33},{2,18}... | collective-permute-start | bytes 2359304 | tf_op jit(solution)/shard_map/ppermute | solution.py:65
  79.9 57.8 %collective-permute-start.6 = (f32[1536,128]{1,0:T(8,128)S(1)}, f32[1536,128]{1,0:T(8,128)S(1)}, u32[]{:S(2)}, u32[]{:S(2)}) collective-permute-start(f32[1536,128]{1,0:T(8,128)S(1)} %collective-permute-done.5), channel_id=1, source_target_pairs={{0,192},{64,0},{128,64},{192,128},{1,193},{65,1},{129,65},{193,129... | collective-permute-start | bytes 2359304 | tf_op jit(solution)/shard_map/ppermute | solution.py:81
  110.3 37.5 %collective-permute-start.4 = (f32[1536,128]{1,0:T(8,128)}, f32[1536,128]{1,0:T(8,128)S(1)}, u32[]{:S(2)}, u32[]{:S(2)}) collective-permute-start(f32[1536,128]{1,0:T(8,128)} %collective-permute-done.2), channel_id=1, source_target_pairs={{0,64},{64,128},{128,192},{192,0},{1,65},{65,129},{129,193},{193,1... | collective-permute-start | bytes 2359304 | tf_op jit(solution)/shard_map/ppermute | solution.py:81
  127.1 24.0 %collective-permute-start.13 = (f32[1536,128]{1,0:T(8,128)S(1)}, f32[1536,128]{1,0:T(8,128)S(1)}, u32[]{:S(2)}, u32[]{:S(2)}) collective-permute-start(f32[1536,128]{1,0:T(8,128)S(1)} %collective-permute-done.11), channel_id=1, source_target_pairs={{0,16},{16,0},{32,48},{48,32},{1,17},{17,1},{33,49},{49,33},{2,18}... | collective-permute-start | bytes 2359304 | tf_op jit(solution)/shard_map/ppermute | solution.py:69
  135.9 24.9 %collective-permute-start.12 = (f32[1536,128]{1,0:T(8,128)S(1)}, f32[1536,128]{1,0:T(8,128)S(1)}, u32[]{:S(2)}, u32[]{:S(2)}) collective-permute-start(f32[1536,128]{1,0:T(8,128)S(1)} %collective-permute-done.8), channel_id=1, source_target_pairs={{0,32},{16,48},{32,0},{48,16},{1,33},{17,49},{33,1},{49,17},{2,34}... | collective-permute-start | bytes 2359304 | tf_op jit(solution)/shard_map/ppermute | solution.py:69
  167.1 2.8 %collective-permute-start.14 = (f32[8,128,128]{2,1,0:T(8,128)S(1)}, f32[8,128,128]{2,1,0:T(8,128)S(1)}, u32[]{:S(2)}, u32[]{:S(2)}) collective-permute-start(f32[8,128,128]{2,1,0:T(8,128)S(1)} %gather_fusion.1), channel_id=1, source_target_pairs={{0,1},{1,0},{2,3},{3,2},{4,5},{5,4},{6,7},{7,6},{8,9},{9,8},{10,11... | collective-permute-start | bytes 1572872 | tf_op jit(solution)/shard_map/ppermute | solution.py:190

commit v4 on v3

--- a/solution.py
+++ b/solution.py
@@ -219,14 +219,29 @@
     rows = square_gather(panel, "c")
     cols = ring_gather(snapshots, "r")
     relayed_row, relayed_col = len(rows) - 1, len(cols) // 2
+    half = node_rows // 2
+
+    def halves_of(block):
+        return block if isinstance(block, list) else [block[:half], block[half:]]
+
+    row_halves = [halves_of(a) for a in rows]
+    col_halves = [halves_of(b) for b in cols]
+    plain_cols = [k2 for k2 in range(side) if k2 != relayed_col]
+    far = sum(
+        contract(jnp.concatenate([r[p] for r in row_halves], 1), col_halves[relayed_col][p])
+        for p in range(2)
+    )
+    corner = sum(
+        contract(row_halves[relayed_row][p], jnp.concatenate([col_halves[k][p] for k in plain_cols], 1))
+        for p in range(2)
+    )
 
     def product(k1, k2):
-        if k1 == relayed_row or k2 == relayed_col:
-            half = node_rows // 2
-            a, b = rows[k1], cols[k2]
-            a = a if isinstance(a, list) else [a[:half], a[half:]]
-            b = b if isinstance(b, list) else [b[:half], b[half:]]
-            return contract(a[0], b[0]) + contract(a[1], b[1])
+        if k2 == relayed_col:
+            return far[k1 * group_cols : (k1 + 1) * group_cols]
+        if k1 == relayed_row:
+            at = plain_cols.index(k2) * group_cols
+            return corner[:, at : at + group_cols]
         return contract(joined(rows[k1]), joined(cols[k2]))
 
     blocks = jnp.stack(

time: 191 us -> 194 us (1.016)
  starting transfers between devices: 26.7 us -> 47.5 us
  waiting for transfers between devices: 105 us -> 90.4 us
  matrix products: 27.1 us -> 23.3 us
    ppermute x1, waiting for transfers between devices: 0.01 us -> 27.8 us  [ring_gather(): left_low = lax.ppermute(block[:half], axis, up)]
    ppermute x1, waiting for transfers between devices: 23.7 us -> 0.36 us  [ring_gather(): right_low = lax.ppermute(block[:half], axis, down)]
    ppermute x1, starting transfers between devices: 0.74 us -> 21.5 us  [square_gather(): z_high = lax.ppermute(block[half:], axis, to_z)]
    ppermute x1, waiting for transfers between devices: 19.7 us -> 0.01 us  [ring_gather(): right_high = lax.ppermute(block[half:], axis, down)]
    ppermute x2, waiting for transfers between devices: 6.36 us -> 16.6 us  [square_gather(): corner = [lax.ppermute(x_low, axis, to_z), lax.ppermute(z_high, axis, to_x)]]
    ppermute x1, waiting for transfers between devices: 16.8 us -> 8.43 us  [square_gather(): z_low = lax.ppermute(block[:half], axis, to_z)]
    ppermute x1, starting transfers between devices: 0.01 us -> 4.19 us  [ring_gather(): lax.ppermute(left_low, axis, up)]
    dot_general x23 -> x13, matrix products: 27.1 us -> 23.3 us  [contract(): lax.dot_general(left, right, (((0,), (0,)), ((), ())), precision=lax.Prec...]
  transfers between devices with their start and end apart: 15 -> 15, of which waited for: 9 -> 10; matrix products, arithmetic and copies ran while one was open for 15% -> 13% of each run, Pallas kernels for 0% -> 0%
where the time goes in v4:
time: 194 us; the launch traced here: 190 us
  waiting for transfers between devices  90.4 us (47%)
  starting transfers between devices  47.5 us (24%)
  matrix products  23.3 us (12%)
  Pallas kernels  15.7 us (8%)
  local copies, waits for them, and re-layouts  8.92 us (5%)
  other arithmetic  4 us (2%)
    ppermute x1, waiting for transfers between devices, ring_gather(): left_low = lax.ppermute(block[:half], axis, up)  27.8 us
    ppermute x1, waiting for transfers between devices, square_gather(): z_high = lax.ppermute(block[half:], axis, to_z)  24.2 us
    dot_general x13, matrix products, contract(): lax.dot_general(left, right, (((0,), (0,)), ((), ())), precision=lax.Prec...  23.3 us
    ppermute x1, starting transfers between devices, square_gather(): z_high = lax.ppermute(block[half:], axis, to_z)  21.5 us
    ppermute x2, waiting for transfers between devices, square_gather(): corner = [lax.ppermute(x_low, axis, to_z), lax.ppermute(z_high, axis, to_x)]  16.6 us
    pallas_call x1, Pallas kernels, scatter_to_owners(): pl.pallas_call(functools.partial(owners_kernel, side, tiles), out_shape=j...  15.7 us
    ppermute x1, waiting for transfers between devices, square_gather(): z_low = lax.ppermute(block[:half], axis, to_z)  8.43 us
    ppermute x1, waiting for transfers between devices, ring_gather(): lax.ppermute(left_low, axis, up)  7.13 us
  transfers between devices with their start and end apart: 15, of which 10 were waited for; matrix products, arithmetic and copies ran while one was open for 13% of the time, Pallas kernels for 0%

profile of v4, /device:TPU:31, one launch (start us, length us, event | category | flops | bytes accessed | tf_op | source)
XLA Modules:
  0.0 190.1 jit_solution(4223245543455482563)
XLA Ops:
  0.0 2.8 %fusion.61 = (f32[1536,128]{1,0:T(8,128)}, f32[1536,128]{1,0:T(8,128)}) fusion(f32[3072,128]{1,0:T(8,128)} %param.3), kind=kLoop, calls=%fused_computation.138 | loop fusion | bytes 3145728 | tf_op jit(solution)/shard_map/slice | solution.py:77
  2.8 3.0 %collective-permute-start.3 = (f32[1536,128]{1,0:T(8,128)}, f32[1536,128]{1,0:T(8,128)}, u32[]{:S(2)}, u32[]{:S(2)}) collective-permute-start(f32[1536,128]{1,0:T(8,128)} %get-tuple-element.11), channel_id=1, source_target_pairs={{0,64},{64,128},{128,192},{192,0},{1,65},{65,129},{129,193},{193,1... | collective-permute-start | bytes 2359304 | tf_op jit(solution)/shard_map/ppermute | solution.py:79
  5.8 3.0 %collective-permute-start.11 = (f32[1536,128]{1,0:T(8,128)}, f32[1536,128]{1,0:T(8,128)}, u32[]{:S(2)}, u32[]{:S(2)}) collective-permute-start(f32[1536,128]{1,0:T(8,128)} %get-tuple-element.11), channel_id=1, source_target_pairs={{0,192},{64,0},{128,64},{192,128},{1,193},{65,1},{129,65},{193,129... | collective-permute-start | bytes 2359304 | tf_op jit(solution)/shard_map/ppermute | solution.py:78
  10.0 2.4 %collective-permute-start.13 = (f32[1536,128]{1,0:T(8,128)}, f32[1536,128]{1,0:T(8,128)S(1)}, u32[]{:S(2)}, u32[]{:S(2)}) collective-permute-start(f32[1536,128]{1,0:T(8,128)} %get-tuple-element.10), channel_id=1, source_target_pairs={{0,192},{64,0},{128,64},{192,128},{1,193},{65,1},{129,65},{193,129... | collective-permute-start | bytes 2359304 | tf_op jit(solution)/shard_map/ppermute | solution.py:80
  13.1 3.4 %collective-permute-start = (f32[512,128]{1,0:T(8,128)}, f32[512,128]{1,0:T(8,128)S(1)}, u32[]{:S(2)}, u32[]{:S(2)}) collective-permute-start(f32[512,128]{1,0:T(8,128)} %slice.77), channel_id=1, source_target_pairs={{1,0},{2,1},{3,2},{4,3},{5,4},{6,5},{7,6},{8,7},{9,8},{10,9},{11,1... | collective-permute-start | bytes 786440 | tf_op jit(solution)/shard_map/ppermute | solution.py:16
  18.6 1.3 add_multiply_fusion.2
  19.9 1.3 collective-permute-start.1
  21.9 3.8 %collective-permute-done.1 = f32[512,128]{1,0:T(8,128)S(1)} collective-permute-done((f32[512,128]{1,0:T(8,128)S(1)}, f32[512,128]{1,0:T(8,128)S(1)}, u32[]{:S(2)}, u32[]{:S(2)}) %collective-permute-start.1) | collective-permute-done | bytes 262176 | tf_op jit(solution)/shard_map/ppermute | solution.py:16
  27.1 1.5 convolution_bitcast_fusion.8
  28.5 27.8 %collective-permute-done.2 = f32[1536,128]{1,0:T(8,128)S(1)} collective-permute-done((f32[1536,128]{1,0:T(8,128)}, f32[1536,128]{1,0:T(8,128)S(1)}, u32[]{:S(2)}, u32[]{:S(2)}) %collective-permute-start.2) | collective-permute-done | bytes 786464 | tf_op jit(solution)/shard_map/ppermute | solution.py:77
  56.3 21.5 %collective-permute-start.9 = (f32[1536,128]{1,0:T(8,128)S(1)}, f32[1536,128]{1,0:T(8,128)S(1)}, u32[]{:S(2)}, u32[]{:S(2)}) collective-permute-start(f32[1536,128]{1,0:T(8,128)S(1)} %bitcast.84), channel_id=1, source_target_pairs={{0,32},{16,48},{32,0},{48,16},{1,33},{17,49},{33,1},{49,17},{2,34}... | collective-permute-start | bytes 2359304 | tf_op jit(solution)/shard_map/ppermute | solution.py:66
  79.6 1.2 constant_dynamic-update-slice_fusion.2
  80.8 1.5 convolution_bitcast_fusion.6
  82.3 2.6 %collective-permute-start.12 = (f32[1536,128]{1,0:T(8,128)}, f32[1536,128]{1,0:T(8,128)S(1)}, u32[]{:S(2)}, u32[]{:S(2)}) collective-permute-start(f32[1536,128]{1,0:T(8,128)} %collective-permute-done.11), channel_id=1, source_target_pairs={{0,192},{64,0},{128,64},{192,128},{1,193},{65,1},{129,65},{193,129... | collective-permute-start | bytes 2359304 | tf_op jit(solution)/shard_map/ppermute | solution.py:81
  86.1 1.5 convolution_bitcast_fusion.7
  87.6 24.2 %collective-permute-done.9 = f32[1536,128]{1,0:T(8,128)S(1)} collective-permute-done((f32[1536,128]{1,0:T(8,128)S(1)}, f32[1536,128]{1,0:T(8,128)S(1)}, u32[]{:S(2)}, u32[]{:S(2)}) %collective-permute-start.9) | collective-permute-done | bytes 786464 | tf_op jit(solution)/shard_map/ppermute | solution.py:66
  111.7 4.2 %collective-permute-start.7 = (f32[1536,128]{1,0:T(8,128)S(1)}, f32[1536,128]{1,0:T(8,128)S(1)}, u32[]{:S(2)}, u32[]{:S(2)}) collective-permute-start(f32[1536,128]{1,0:T(8,128)S(1)} %collective-permute-done.2), channel_id=1, source_target_pairs={{0,64},{64,128},{128,192},{192,0},{1,65},{65,129},{129,193},{193,1... | collective-permute-start | bytes 2359304 | tf_op jit(solution)/shard_map/ppermute | solution.py:81
  117.2 1.5 convolution_bitcast_fusion.4
  118.7 1.5 convolution_bitcast_fusion.3
  120.1 8.4 %collective-permute-done.5 = f32[1536,128]{1,0:T(8,128)S(1)} collective-permute-done((f32[1536,128]{1,0:T(8,128)S(1)}, f32[1536,128]{1,0:T(8,128)S(1)}, u32[]{:S(2)}, u32[]{:S(2)}) %collective-permute-start.5) | collective-permute-done | bytes 786464 | tf_op jit(solution)/shard_map/ppermute | solution.py:68
  128.7 1.5 convolution_bitcast_fusion.5
  130.2 1.5 convolution_bitcast_fusion.1
  132.0 1.5 convolution_bitcast_fusion
  133.5 1.5 convolution_bitcast_fusion.2
  135.6 2.6 %fusion.22 = f32[128,384]{1,0:T(8,128)S(1)} fusion(f32[1536,128]{1,0:T(8,128)S(1)} %collective-permute-done.10, f32[1536,128]{1,0:T(8,128)} %collective-permute-done.11, f32[1536,128]{1,0:T(8,128)} %collective-permute-done.3, f32[1536,128]{1,0:T(8,128)} %get-tuple-element.11), kind=kOutput, calls=%fused_computation.26 | convolution fusion | flops 454164480 | bytes 3342336 | tf_op jit(solution)/shard_map/dot_general | solution.py:49
  138.2 2.6 %fusion.8 = f32[512,128]{1,0:T(8,128)S(1)} fusion(f32[1536,128]{1,0:T(8,128)S(1)} %collective-permute-done.12, f32[1536,128]{1,0:T(8,128)S(1)} %collective-permute-done.10, f32[1536,128]{1,0:T(8,128)S(1)} %collective-permute-done.9, f32[1536,128]{1,0:T(8,128)S(1)} %collective-permute-done.8, f32[1536,128]{1,0:T(8,128)S(1)} %bitcast.85), kind=kOutput, calls=%fused_computation.10 | convolution fusion | flops 606339072 | bytes 4194304 | tf_op jit(solution)/shard_map/dot_general | solution.py:49
  140.9 7.1 %collective-permute-done.7 = f32[1536,128]{1,0:T(8,128)S(1)} collective-permute-done((f32[1536,128]{1,0:T(8,128)S(1)}, f32[1536,128]{1,0:T(8,128)S(1)}, u32[]{:S(2)}, u32[]{:S(2)}) %collective-permute-start.7) | collective-permute-done | bytes 786464 | tf_op jit(solution)/shard_map/ppermute | solution.py:81
  148.0 15.9 %collective-permute-done.6 = f32[1536,128]{1,0:T(8,128)S(1)} collective-permute-done((f32[1536,128]{1,0:T(8,128)S(1)}, f32[1536,128]{1,0:T(8,128)S(1)}, u32[]{:S(2)}, u32[]{:S(2)}) %collective-permute-start.6) | collective-permute-done | bytes 786464 | tf_op jit(solution)/shard_map/ppermute | solution.py:69
  163.9 2.7 %fusion.29 = f32[512,128]{1,0:T(8,128)S(1)} fusion(f32[512,128]{1,0:T(8,128)S(1)} %fusion.8, f32[1536,128]{1,0:T(8,128)S(1)} %collective-permute-done.7, f32[1536,128]{1,0:T(8,128)S(1)} %collective-permute-done.6, f32[1536,128]{1,0:T(8,128)S(1)} %collective-permute-done.5, f32[1536,128]{1,0:T(8,128)S(1)} %collective-permute-done.4, f32[1536,128]{1,0:T(8,128)S(1)} %bitcast.88), kind=kOutput, calls=%fused_computation.44 | convolution fusion | flops 606404608 | bytes 4456448 | tf_op jit(solution)/shard_map/dot_general | solution.py:49
  166.6 2.1 %fusion.32 = f32[128,384]{1,0:T(8,128)S(1)} fusion(f32[128,384]{1,0:T(8,128)S(1)} %fusion.22, f32[1536,128]{1,0:T(8,128)S(1)} %collective-permute-done.6, f32[1536,128]{1,0:T(8,128)S(1)} %collective-permute-done.13, f32[1536,128]{1,0:T(8,128)S(1)} %collective-permute-done.2, f32[1536,128]{1,0:T(8,128)} %get-tuple-element.10), kind=kOutput, calls=%fused_computation.45 | convolution fusion | flops 454213632 | bytes 3538944 | tf_op jit(solution)/shard_map/dot_general | solution.py:49
  173.0 15.7 %shard_map.37 = f32[128,128]{1,0:T(8,128)} custom-call(f32[8,128,128]{2,1,0:T(8,128)} %add_multiply_fusion.4.part_ref), custom_call_target="tpu_custom_call" | custom-call | tf_op jit(solution)/shard_map/pallas_call | solution.py:191
  188.6 1.5 copy.9
  (51 shorter events, 15.4 us)
Async XLA Ops:
  0.0 12.4 %copy-start = (f32[3072,128]{1,0:T(8,128)S(1)}, f32[3072,128]{1,0:T(8,128)}, u32[]{:S(2)}) copy-start(f32[3072,128]{1,0:T(8,128)} %param.3) | copy-start | bytes 4718596
  0.0 16.5 %copy-start.1 = (s32[6,512]{1,0:T(8,128)S(1)}, s32[6,512]{1,0:T(8,128)}, u32[]{:S(2)}) copy-start(s32[6,512]{1,0:T(8,128)} %param.4) | copy-start | bytes 36868
  0.0 16.5 %copy-start.2 = (f32[8]{0:T(128)S(1)}, f32[8]{0:T(128)}, u32[]{:S(2)}) copy-start(f32[8]{0:T(128)} %param.5) | copy-start | bytes 100
  2.8 79.5 %collective-permute-start.3 = (f32[1536,128]{1,0:T(8,128)}, f32[1536,128]{1,0:T(8,128)}, u32[]{:S(2)}, u32[]{:S(2)}) collective-permute-start(f32[1536,128]{1,0:T(8,128)} %get-tuple-element.11), channel_id=1, source_target_pairs={{0,64},{64,128},{128,192},{192,0},{1,65},{65,129},{129,193},{193,1... | collective-permute-start | bytes 2359304 | tf_op jit(solution)/shard_map/ppermute | solution.py:79
  5.8 73.7 %collective-permute-start.11 = (f32[1536,128]{1,0:T(8,128)}, f32[1536,128]{1,0:T(8,128)}, u32[]{:S(2)}, u32[]{:S(2)}) collective-permute-start(f32[1536,128]{1,0:T(8,128)} %get-tuple-element.11), channel_id=1, source_target_pairs={{0,192},{64,0},{128,64},{192,128},{1,193},{65,1},{129,65},{193,129... | collective-permute-start | bytes 2359304 | tf_op jit(solution)/shard_map/ppermute | solution.py:78
  8.8 47.6 %collective-permute-start.2 = (f32[1536,128]{1,0:T(8,128)}, f32[1536,128]{1,0:T(8,128)S(1)}, u32[]{:S(2)}, u32[]{:S(2)}) collective-permute-start(f32[1536,128]{1,0:T(8,128)} %get-tuple-element.10), channel_id=1, source_target_pairs={{0,64},{64,128},{128,192},{192,0},{1,65},{65,129},{129,193},{193,1... | collective-permute-start | bytes 2359304 | tf_op jit(solution)/shard_map/ppermute | solution.py:77
  10.0 68.3 %collective-permute-start.13 = (f32[1536,128]{1,0:T(8,128)}, f32[1536,128]{1,0:T(8,128)S(1)}, u32[]{:S(2)}, u32[]{:S(2)}) collective-permute-start(f32[1536,128]{1,0:T(8,128)} %get-tuple-element.10), channel_id=1, source_target_pairs={{0,192},{64,0},{128,64},{192,128},{1,193},{65,1},{129,65},{193,129... | collective-permute-start | bytes 2359304 | tf_op jit(solution)/shard_map/ppermute | solution.py:80
  13.1 4.8 %collective-permute-start = (f32[512,128]{1,0:T(8,128)}, f32[512,128]{1,0:T(8,128)S(1)}, u32[]{:S(2)}, u32[]{:S(2)}) collective-permute-start(f32[512,128]{1,0:T(8,128)} %slice.77), channel_id=1, source_target_pairs={{1,0},{2,1},{3,2},{4,3},{5,4},{6,5},{7,6},{8,7},{9,8},{10,9},{11,1... | collective-permute-start | bytes 786440 | tf_op jit(solution)/shard_map/ppermute | solution.py:16
  19.9 5.8 %collective-permute-start.1 = (f32[512,128]{1,0:T(8,128)S(1)}, f32[512,128]{1,0:T(8,128)S(1)}, u32[]{:S(2)}, u32[]{:S(2)}) collective-permute-start(f32[512,128]{1,0:T(8,128)S(1)} %add_bitcast_fusion), channel_id=1, source_target_pairs={{0,1},{1,2},{2,3},{3,4},{4,5},{5,6},{6,7},{7,8},{8,9},{9,10},{10,1... | collective-permute-start | bytes 786440 | tf_op jit(solution)/shard_map/ppermute | solution.py:16
  25.7 91.4 %collective-permute-start.8 = (f32[1536,128]{1,0:T(8,128)S(1)}, f32[1536,128]{1,0:T(8,128)S(1)}, u32[]{:S(2)}, u32[]{:S(2)}) collective-permute-start(f32[1536,128]{1,0:T(8,128)S(1)} %bitcast.83), channel_id=1, source_target_pairs={{0,16},{16,0},{32,48},{48,32},{1,17},{17,1},{33,49},{49,33},{2,18}... | collective-permute-start | bytes 2359304 | tf_op jit(solution)/shard_map/ppermute | solution.py:67
  56.3 55.4 %collective-permute-start.9 = (f32[1536,128]{1,0:T(8,128)S(1)}, f32[1536,128]{1,0:T(8,128)S(1)}, u32[]{:S(2)}, u32[]{:S(2)}) collective-permute-start(f32[1536,128]{1,0:T(8,128)S(1)} %bitcast.84), channel_id=1, source_target_pairs={{0,32},{16,48},{32,0},{48,16},{1,33},{17,49},{33,1},{49,17},{2,34}... | collective-permute-start | bytes 2359304 | tf_op jit(solution)/shard_map/ppermute | solution.py:66
  78.3 37.6 %collective-permute-start.4 = (f32[1536,128]{1,0:T(8,128)S(1)}, f32[1536,128]{1,0:T(8,128)S(1)}, u32[]{:S(2)}, u32[]{:S(2)}) collective-permute-start(f32[1536,128]{1,0:T(8,128)S(1)} %bitcast.86), channel_id=1, source_target_pairs={{0,16},{16,0},{32,48},{48,32},{1,17},{17,1},{33,49},{49,33},{2,18}... | collective-permute-start | bytes 2359304 | tf_op jit(solution)/shard_map/ppermute | solution.py:65
  79.5 49.1 %collective-permute-start.5 = (f32[1536,128]{1,0:T(8,128)S(1)}, f32[1536,128]{1,0:T(8,128)S(1)}, u32[]{:S(2)}, u32[]{:S(2)}) collective-permute-start(f32[1536,128]{1,0:T(8,128)S(1)} %bitcast.87), channel_id=1, source_target_pairs={{0,32},{16,48},{32,0},{48,16},{1,33},{17,49},{33,1},{49,17},{2,34}... | collective-permute-start | bytes 2359304 | tf_op jit(solution)/shard_map/ppermute | solution.py:68
  82.3 55.9 %collective-permute-start.12 = (f32[1536,128]{1,0:T(8,128)}, f32[1536,128]{1,0:T(8,128)S(1)}, u32[]{:S(2)}, u32[]{:S(2)}) collective-permute-start(f32[1536,128]{1,0:T(8,128)} %collective-permute-done.11), channel_id=1, source_target_pairs={{0,192},{64,0},{128,64},{192,128},{1,193},{65,1},{129,65},{193,129... | collective-permute-start | bytes 2359304 | tf_op jit(solution)/shard_map/ppermute | solution.py:81
  111.7 36.3 %collective-permute-start.7 = (f32[1536,128]{1,0:T(8,128)S(1)}, f32[1536,128]{1,0:T(8,128)S(1)}, u32[]{:S(2)}, u32[]{:S(2)}) collective-permute-start(f32[1536,128]{1,0:T(8,128)S(1)} %collective-permute-done.2), channel_id=1, source_target_pairs={{0,64},{64,128},{128,192},{192,0},{1,65},{65,129},{129,193},{193,1... | collective-permute-start | bytes 2359304 | tf_op jit(solution)/shard_map/ppermute | solution.py:81
  115.9 19.7 %collective-permute-start.10 = (f32[1536,128]{1,0:T(8,128)S(1)}, f32[1536,128]{1,0:T(8,128)S(1)}, u32[]{:S(2)}, u32[]{:S(2)}) collective-permute-start(f32[1536,128]{1,0:T(8,128)S(1)} %collective-permute-done.9), channel_id=1, source_target_pairs={{0,16},{16,0},{32,48},{48,32},{1,17},{17,1},{33,49},{49,33},{2,18}... | collective-permute-start | bytes 2359304 | tf_op jit(solution)/shard_map/ppermute | solution.py:69
  131.6 32.2 %collective-permute-start.6 = (f32[1536,128]{1,0:T(8,128)S(1)}, f32[1536,128]{1,0:T(8,128)S(1)}, u32[]{:S(2)}, u32[]{:S(2)}) collective-permute-start(f32[1536,128]{1,0:T(8,128)S(1)} %collective-permute-done.4), channel_id=1, source_target_pairs={{0,32},{16,48},{32,0},{48,16},{1,33},{17,49},{33,1},{49,17},{2,34}... | collective-permute-start | bytes 2359304 | tf_op jit(solution)/shard_map/ppermute | solution.py:69
  169.5 2.6 %collective-permute-start.14 = (f32[8,128,128]{2,1,0:T(8,128)S(1)}, f32[8,128,128]{2,1,0:T(8,128)S(1)}, u32[]{:S(2)}, u32[]{:S(2)}) collective-permute-start(f32[8,128,128]{2,1,0:T(8,128)S(1)} %gather_fusion.1), channel_id=1, source_target_pairs={{0,1},{1,0},{2,3},{3,2},{4,5},{5,4},{6,7},{7,6},{8,9},{9,8},{10,11... | collective-permute-start | bytes 1572872 | tf_op jit(solution)/shard_map/ppermute | solution.py:190

commit v5 on v3

--- a/solution.py
+++ b/solution.py
@@ -91,7 +91,7 @@
     return a + b - 2 * both
 
 
-def owners_kernel(side, tiles, part_ref, out_ref, slots, send_sems, recv_sems):
+def owners_kernel(side, tiles, part_ref, slots, send_sems, recv_sems):
     me_r, me_c, me_t = lax.axis_index("r"), lax.axis_index("c"), lax.axis_index("mesh")
     halves = tiles // 2
     parity = me_t % 2
@@ -170,11 +170,6 @@
         def _():
             copy.wait_send()
 
-    acc = slots[0]
-    for source in range(1, halves):
-        acc = acc + slots[source]
-    out_ref[...] = acc
-
 
 def scatter_to_owners(blocks, side, tiles, scale):
     width = blocks.shape[-1]
@@ -188,18 +183,18 @@
 
     parity = me_t % 2
     kept = (pieces(parity) + lax.ppermute(pieces(1 - parity), "mesh", pairs(tiles, lambda i: i ^ 1))) / scale
-    return pl.pallas_call(
+    slots = pl.pallas_call(
         functools.partial(owners_kernel, side, tiles),
-        out_shape=jax.ShapeDtypeStruct((width, width), jnp.float32),
+        out_shape=jax.ShapeDtypeStruct((halves, width, width), jnp.float32),
         in_specs=[pl.BlockSpec(memory_space=pltpu.VMEM)],
         out_specs=pl.BlockSpec(memory_space=pltpu.VMEM),
         scratch_shapes=[
-            pltpu.VMEM((halves, width, width), jnp.float32),
             pltpu.SemaphoreType.DMA((halves,)),
             pltpu.SemaphoreType.DMA((halves,)),
         ],
         compiler_params=pltpu.CompilerParams(collective_id=0, has_side_effects=True),
     )(kept)
+    return jnp.sum(slots, axis=0)
 
 
 def local(snapshots, region_ids, conductivity):

time: 191 us -> 192 us (level)
    unnamed x11 -> x10, local copies, waits for them, and re-layouts: 3.96 us -> 2.48 us
where the time goes in v5:
time: 192 us; the launch traced here: 188 us
  waiting for transfers between devices  105 us (55%)
  matrix products  27.1 us (14%)
  starting transfers between devices  26.7 us (14%)
  Pallas kernels  15.8 us (8%)
  local copies, waits for them, and re-layouts  7.43 us (4%)
  other arithmetic  5.72 us (3%)
    dot_general x23, matrix products, contract(): lax.dot_general(left, right, (((0,), (0,)), ((), ())), precision=lax.Prec...  27.1 us
    ppermute x1, waiting for transfers between devices, square_gather(): z_high = lax.ppermute(block[half:], axis, to_z)  24.2 us
    ppermute x1, waiting for transfers between devices, ring_gather(): right_low = lax.ppermute(block[:half], axis, down)  23.7 us
    ppermute x1, waiting for transfers between devices, ring_gather(): right_high = lax.ppermute(block[half:], axis, down)  19.7 us
    ppermute x1, waiting for transfers between devices, square_gather(): z_low = lax.ppermute(block[:half], axis, to_z)  16.8 us
    pallas_call x1, Pallas kernels, scatter_to_owners(): pl.pallas_call(functools.partial(owners_kernel, side, tiles), out_shape=j...  15.8 us
    ppermute x1, waiting for transfers between devices, ring_gather(): lax.ppermute(left_low, axis, up)  8.36 us
    ppermute x2, waiting for transfers between devices, square_gather(): corner = [lax.ppermute(x_low, axis, to_z), lax.ppermute(z_high, axis, to_x)]  6.36 us
  transfers between devices with their start and end apart: 15, of which 9 were waited for; matrix products, arithmetic and copies ran while one was open for 15% of the time, Pallas kernels for 0%

profile of v5, /device:TPU:31, one launch (start us, length us, event | category | flops | bytes accessed | tf_op | source)
XLA Modules:
  0.0 188.3 jit_solution(1255261127436749539)
XLA Ops:
  0.0 2.8 %fusion.33 = (f32[1536,128]{1,0:T(8,128)}, f32[1536,128]{1,0:T(8,128)}) fusion(f32[3072,128]{1,0:T(8,128)} %param.3), kind=kLoop, calls=%fused_computation.114 | loop fusion | bytes 3145728 | tf_op jit(solution)/shard_map/slice | solution.py:77
  2.8 6.0 %collective-permute-start.7 = (f32[1536,128]{1,0:T(8,128)}, f32[1536,128]{1,0:T(8,128)}, u32[]{:S(2)}, u32[]{:S(2)}) collective-permute-start(f32[1536,128]{1,0:T(8,128)} %get-tuple-element.10), channel_id=1, source_target_pairs={{0,192},{64,0},{128,64},{192,128},{1,193},{65,1},{129,65},{193,129... | collective-permute-start | bytes 2359304 | tf_op jit(solution)/shard_map/ppermute | solution.py:80
  8.8 3.6 %collective-permute-start.5 = (f32[1536,128]{1,0:T(8,128)}, f32[1536,128]{1,0:T(8,128)S(1)}, u32[]{:S(2)}, u32[]{:S(2)}) collective-permute-start(f32[1536,128]{1,0:T(8,128)} %get-tuple-element.11), channel_id=1, source_target_pairs={{0,192},{64,0},{128,64},{192,128},{1,193},{65,1},{129,65},{193,129... | collective-permute-start | bytes 2359304 | tf_op jit(solution)/shard_map/ppermute | solution.py:78
  13.1 3.4 %collective-permute-start = (f32[512,128]{1,0:T(8,128)}, f32[512,128]{1,0:T(8,128)S(1)}, u32[]{:S(2)}, u32[]{:S(2)}) collective-permute-start(f32[512,128]{1,0:T(8,128)} %slice.56), channel_id=1, source_target_pairs={{1,0},{2,1},{3,2},{4,3},{5,4},{6,5},{7,6},{8,7},{9,8},{10,9},{11,1... | collective-permute-start | bytes 786440 | tf_op jit(solution)/shard_map/ppermute | solution.py:16
  18.6 1.3 add_multiply_fusion.2
  19.9 1.3 collective-permute-start.1
  21.9 3.8 %collective-permute-done.1 = f32[512,128]{1,0:T(8,128)S(1)} collective-permute-done((f32[512,128]{1,0:T(8,128)S(1)}, f32[512,128]{1,0:T(8,128)S(1)}, u32[]{:S(2)}, u32[]{:S(2)}) %collective-permute-start.1) | collective-permute-done | bytes 262176 | tf_op jit(solution)/shard_map/ppermute | solution.py:16
  26.6 1.5 convolution_bitcast_fusion.8
  28.2 23.7 %collective-permute-done.7 = f32[1536,128]{1,0:T(8,128)} collective-permute-done((f32[1536,128]{1,0:T(8,128)}, f32[1536,128]{1,0:T(8,128)}, u32[]{:S(2)}, u32[]{:S(2)}) %collective-permute-start.7) | collective-permute-done | bytes 786464 | tf_op jit(solution)/shard_map/ppermute | solution.py:80
  53.0 1.2 constant_dynamic-update-slice_fusion.3
  54.2 19.7 %collective-permute-done.5 = f32[1536,128]{1,0:T(8,128)S(1)} collective-permute-done((f32[1536,128]{1,0:T(8,128)}, f32[1536,128]{1,0:T(8,128)S(1)}, u32[]{:S(2)}, u32[]{:S(2)}) %collective-permute-start.5) | collective-permute-done | bytes 786464 | tf_op jit(solution)/shard_map/ppermute | solution.py:78
  73.9 2.0 %collective-permute-start.10 = (f32[1536,128]{1,0:T(8,128)S(1)}, f32[1536,128]{1,0:T(8,128)S(1)}, u32[]{:S(2)}, u32[]{:S(2)}) collective-permute-start(f32[1536,128]{1,0:T(8,128)S(1)} %bitcast.106), channel_id=1, source_target_pairs={{0,32},{16,48},{32,0},{48,16},{1,33},{17,49},{33,1},{49,17},{2,34}... | collective-permute-start | bytes 2359304 | tf_op jit(solution)/shard_map/ppermute | solution.py:68
  76.0 1.5 convolution_bitcast_fusion.6
  77.5 1.2 collective-permute-start.8
  78.7 1.2 constant_dynamic-update-slice_fusion.1
  79.9 4.6 %collective-permute-start.6 = (f32[1536,128]{1,0:T(8,128)S(1)}, f32[1536,128]{1,0:T(8,128)S(1)}, u32[]{:S(2)}, u32[]{:S(2)}) collective-permute-start(f32[1536,128]{1,0:T(8,128)S(1)} %collective-permute-done.5), channel_id=1, source_target_pairs={{0,192},{64,0},{128,64},{192,128},{1,193},{65,1},{129,65},{193,129... | collective-permute-start | bytes 2359304 | tf_op jit(solution)/shard_map/ppermute | solution.py:81
  84.6 1.5 convolution_bitcast_fusion.7
  86.0 24.2 %collective-permute-done.11 = f32[1536,128]{1,0:T(8,128)S(1)} collective-permute-done((f32[1536,128]{1,0:T(8,128)S(1)}, f32[1536,128]{1,0:T(8,128)S(1)}, u32[]{:S(2)}, u32[]{:S(2)}) %collective-permute-start.11) | collective-permute-done | bytes 786464 | tf_op jit(solution)/shard_map/ppermute | solution.py:66
  110.3 16.8 %collective-permute-done.10 = f32[1536,128]{1,0:T(8,128)S(1)} collective-permute-done((f32[1536,128]{1,0:T(8,128)S(1)}, f32[1536,128]{1,0:T(8,128)S(1)}, u32[]{:S(2)}, u32[]{:S(2)}) %collective-permute-start.10) | collective-permute-done | bytes 786464 | tf_op jit(solution)/shard_map/ppermute | solution.py:68
  128.4 1.5 convolution_bitcast_fusion
  129.8 1.5 convolution_bitcast_fusion.1
  131.5 1.5 convolution_bitcast_fusion.2
  132.9 1.5 convolution_bitcast_fusion.3
  134.4 1.5 convolution_bitcast_fusion.4
  136.2 1.5 convolution_bitcast_fusion.5
  139.4 8.4 %collective-permute-done.4 = f32[1536,128]{1,0:T(8,128)S(1)} collective-permute-done((f32[1536,128]{1,0:T(8,128)}, f32[1536,128]{1,0:T(8,128)S(1)}, u32[]{:S(2)}, u32[]{:S(2)}) %collective-permute-start.4) | collective-permute-done | bytes 786464 | tf_op jit(solution)/shard_map/ppermute | solution.py:81
  154.5 6.4 %collective-permute-done.12 = f32[1536,128]{1,0:T(8,128)S(1)} collective-permute-done((f32[1536,128]{1,0:T(8,128)S(1)}, f32[1536,128]{1,0:T(8,128)S(1)}, u32[]{:S(2)}, u32[]{:S(2)}) %collective-permute-start.12) | collective-permute-done | bytes 786464 | tf_op jit(solution)/shard_map/ppermute | solution.py:69
  160.8 2.0 %fusion.1 = f32[1,128,128]{2,1,0:T(8,128)S(1)} fusion(f32[128,128]{1,0:T(8,128)S(1)} %fusion.39, f32[1536,128]{1,0:T(8,128)S(1)} %collective-permute-done.12, f32[1536,128]{1,0:T(8,128)} %collective-permute-done.7), kind=kOutput, calls=%fused_computation.17 | convolution fusion | flops 151011328 | bytes 1703936 | tf_op jit(solution)/shard_map/dot_general | solution.py:49
  163.6 2.0 %fusion.3 = f32[1,128,128]{2,1,0:T(8,128)S(1)} fusion(f32[128,128]{1,0:T(8,128)S(1)} %fusion.37, f32[1536,128]{1,0:T(8,128)S(1)} %collective-permute-done.12, f32[1536,128]{1,0:T(8,128)} %collective-permute-done.2), kind=kOutput, calls=%fused_computation.21 | convolution fusion | flops 151011328 | bytes 1703936 | tf_op jit(solution)/shard_map/dot_general | solution.py:49
  167.1 1.2 collective-permute-start.14
  170.8 15.8 %shard_map.37 = f32[8,128,128]{2,1,0:T(8,128)} custom-call(f32[8,128,128]{2,1,0:T(8,128)} %add_multiply_fusion.4.part_ref), custom_call_target="tpu_custom_call" | custom-call | tf_op jit(solution)/shard_map/pallas_call | solution.py:186
  186.6 1.7 reduce_sum.19
  (61 shorter events, 20.3 us)
Async XLA Ops:
  0.0 12.4 %copy-start = (f32[3072,128]{1,0:T(8,128)S(1)}, f32[3072,128]{1,0:T(8,128)}, u32[]{:S(2)}) copy-start(f32[3072,128]{1,0:T(8,128)} %param.3) | copy-start | bytes 4718596
  0.0 16.6 %copy-start.2 = (f32[8]{0:T(128)S(1)}, f32[8]{0:T(128)}, u32[]{:S(2)}) copy-start(f32[8]{0:T(128)} %param.5) | copy-start | bytes 100
  0.0 16.6 %copy-start.1 = (s32[6,512]{1,0:T(8,128)S(1)}, s32[6,512]{1,0:T(8,128)}, u32[]{:S(2)}) copy-start(s32[6,512]{1,0:T(8,128)} %param.4) | copy-start | bytes 36868
  2.8 49.1 %collective-permute-start.7 = (f32[1536,128]{1,0:T(8,128)}, f32[1536,128]{1,0:T(8,128)}, u32[]{:S(2)}, u32[]{:S(2)}) collective-permute-start(f32[1536,128]{1,0:T(8,128)} %get-tuple-element.10), channel_id=1, source_target_pairs={{0,192},{64,0},{128,64},{192,128},{1,193},{65,1},{129,65},{193,129... | collective-permute-start | bytes 2359304 | tf_op jit(solution)/shard_map/ppermute | solution.py:80
  8.8 68.7 %collective-permute-start.2 = (f32[1536,128]{1,0:T(8,128)}, f32[1536,128]{1,0:T(8,128)}, u32[]{:S(2)}, u32[]{:S(2)}) collective-permute-start(f32[1536,128]{1,0:T(8,128)} %get-tuple-element.10), channel_id=1, source_target_pairs={{0,64},{64,128},{128,192},{192,0},{1,65},{65,129},{129,193},{193,1... | collective-permute-start | bytes 2359304 | tf_op jit(solution)/shard_map/ppermute | solution.py:77
  8.8 65.1 %collective-permute-start.5 = (f32[1536,128]{1,0:T(8,128)}, f32[1536,128]{1,0:T(8,128)S(1)}, u32[]{:S(2)}, u32[]{:S(2)}) collective-permute-start(f32[1536,128]{1,0:T(8,128)} %get-tuple-element.11), channel_id=1, source_target_pairs={{0,192},{64,0},{128,64},{192,128},{1,193},{65,1},{129,65},{193,129... | collective-permute-start | bytes 2359304 | tf_op jit(solution)/shard_map/ppermute | solution.py:78
  12.4 67.5 %collective-permute-start.3 = (f32[1536,128]{1,0:T(8,128)}, f32[1536,128]{1,0:T(8,128)S(1)}, u32[]{:S(2)}, u32[]{:S(2)}) collective-permute-start(f32[1536,128]{1,0:T(8,128)} %get-tuple-element.11), channel_id=1, source_target_pairs={{0,64},{64,128},{128,192},{192,0},{1,65},{65,129},{129,193},{193,1... | collective-permute-start | bytes 2359304 | tf_op jit(solution)/shard_map/ppermute | solution.py:79
  13.1 4.8 %collective-permute-start = (f32[512,128]{1,0:T(8,128)}, f32[512,128]{1,0:T(8,128)S(1)}, u32[]{:S(2)}, u32[]{:S(2)}) collective-permute-start(f32[512,128]{1,0:T(8,128)} %slice.56), channel_id=1, source_target_pairs={{1,0},{2,1},{3,2},{4,3},{5,4},{6,5},{7,6},{8,7},{9,8},{10,9},{11,1... | collective-permute-start | bytes 786440 | tf_op jit(solution)/shard_map/ppermute | solution.py:16
  19.9 5.8 %collective-permute-start.1 = (f32[512,128]{1,0:T(8,128)S(1)}, f32[512,128]{1,0:T(8,128)S(1)}, u32[]{:S(2)}, u32[]{:S(2)}) collective-permute-start(f32[512,128]{1,0:T(8,128)S(1)} %add_bitcast_fusion), channel_id=1, source_target_pairs={{0,1},{1,2},{2,3},{3,4},{4,5},{5,6},{6,7},{7,8},{8,9},{9,10},{10,1... | collective-permute-start | bytes 786440 | tf_op jit(solution)/shard_map/ppermute | solution.py:16
  25.7 84.5 %collective-permute-start.11 = (f32[1536,128]{1,0:T(8,128)S(1)}, f32[1536,128]{1,0:T(8,128)S(1)}, u32[]{:S(2)}, u32[]{:S(2)}) collective-permute-start(f32[1536,128]{1,0:T(8,128)S(1)} %bitcast.103), channel_id=1, source_target_pairs={{0,32},{16,48},{32,0},{48,16},{1,33},{17,49},{33,1},{49,17},{2,34}... | collective-permute-start | bytes 2359304 | tf_op jit(solution)/shard_map/ppermute | solution.py:66
  51.9 79.5 %collective-permute-start.9 = (f32[1536,128]{1,0:T(8,128)S(1)}, f32[1536,128]{1,0:T(8,128)S(1)}, u32[]{:S(2)}, u32[]{:S(2)}) collective-permute-start(f32[1536,128]{1,0:T(8,128)S(1)} %bitcast.104), channel_id=1, source_target_pairs={{0,16},{16,0},{32,48},{48,32},{1,17},{17,1},{33,49},{49,33},{2,18}... | collective-permute-start | bytes 2359304 | tf_op jit(solution)/shard_map/ppermute | solution.py:67
  73.9 53.2 %collective-permute-start.10 = (f32[1536,128]{1,0:T(8,128)S(1)}, f32[1536,128]{1,0:T(8,128)S(1)}, u32[]{:S(2)}, u32[]{:S(2)}) collective-permute-start(f32[1536,128]{1,0:T(8,128)S(1)} %bitcast.106), channel_id=1, source_target_pairs={{0,32},{16,48},{32,0},{48,16},{1,33},{17,49},{33,1},{49,17},{2,34}... | collective-permute-start | bytes 2359304 | tf_op jit(solution)/shard_map/ppermute | solution.py:68
  77.5 53.9 %collective-permute-start.8 = (f32[1536,128]{1,0:T(8,128)S(1)}, f32[1536,128]{1,0:T(8,128)S(1)}, u32[]{:S(2)}, u32[]{:S(2)}) collective-permute-start(f32[1536,128]{1,0:T(8,128)S(1)} %bitcast.107), channel_id=1, source_target_pairs={{0,16},{16,0},{32,48},{48,32},{1,17},{17,1},{33,49},{49,33},{2,18}... | collective-permute-start | bytes 2359304 | tf_op jit(solution)/shard_map/ppermute | solution.py:65
  79.9 57.8 %collective-permute-start.6 = (f32[1536,128]{1,0:T(8,128)S(1)}, f32[1536,128]{1,0:T(8,128)S(1)}, u32[]{:S(2)}, u32[]{:S(2)}) collective-permute-start(f32[1536,128]{1,0:T(8,128)S(1)} %collective-permute-done.5), channel_id=1, source_target_pairs={{0,192},{64,0},{128,64},{192,128},{1,193},{65,1},{129,65},{193,129... | collective-permute-start | bytes 2359304 | tf_op jit(solution)/shard_map/ppermute | solution.py:81
  110.3 37.5 %collective-permute-start.4 = (f32[1536,128]{1,0:T(8,128)}, f32[1536,128]{1,0:T(8,128)S(1)}, u32[]{:S(2)}, u32[]{:S(2)}) collective-permute-start(f32[1536,128]{1,0:T(8,128)} %collective-permute-done.2), channel_id=1, source_target_pairs={{0,64},{64,128},{128,192},{192,0},{1,65},{65,129},{129,193},{193,1... | collective-permute-start | bytes 2359304 | tf_op jit(solution)/shard_map/ppermute | solution.py:81
  127.1 24.0 %collective-permute-start.13 = (f32[1536,128]{1,0:T(8,128)S(1)}, f32[1536,128]{1,0:T(8,128)S(1)}, u32[]{:S(2)}, u32[]{:S(2)}) collective-permute-start(f32[1536,128]{1,0:T(8,128)S(1)} %collective-permute-done.11), channel_id=1, source_target_pairs={{0,16},{16,0},{32,48},{48,32},{1,17},{17,1},{33,49},{49,33},{2,18}... | collective-permute-start | bytes 2359304 | tf_op jit(solution)/shard_map/ppermute | solution.py:69
  135.9 24.9 %collective-permute-start.12 = (f32[1536,128]{1,0:T(8,128)S(1)}, f32[1536,128]{1,0:T(8,128)S(1)}, u32[]{:S(2)}, u32[]{:S(2)}) collective-permute-start(f32[1536,128]{1,0:T(8,128)S(1)} %collective-permute-done.8), channel_id=1, source_target_pairs={{0,32},{16,48},{32,0},{48,16},{1,33},{17,49},{33,1},{49,17},{2,34}... | collective-permute-start | bytes 2359304 | tf_op jit(solution)/shard_map/ppermute | solution.py:69
  167.1 2.8 %collective-permute-start.14 = (f32[8,128,128]{2,1,0:T(8,128)S(1)}, f32[8,128,128]{2,1,0:T(8,128)S(1)}, u32[]{:S(2)}, u32[]{:S(2)}) collective-permute-start(f32[8,128,128]{2,1,0:T(8,128)S(1)} %gather_fusion.1), channel_id=1, source_target_pairs={{0,1},{1,0},{2,3},{3,2},{4,5},{5,4},{6,7},{7,6},{8,9},{9,8},{10,11... | collective-permute-start | bytes 1572872 | tf_op jit(solution)/shard_map/ppermute | solution.py:185

commit v6 on v3

--- a/solution.py
+++ b/solution.py
@@ -210,12 +210,14 @@
     field = snapshots.reshape(strip, width, group_cols)
     weight = weights_of(region_ids, conductivity)
     below = passed_along(field[0], "mesh", -1)
-    total = element_terms(field, below, weight)
-    carried = passed_along(total[strip, :width], "mesh", 1)
-    inner = total[:strip, :width]
-    panel = jnp.concatenate([inner[:1] + carried[None], inner[1:]], 0).reshape(
-        node_rows, group_cols
-    )
+    above = passed_along(field[strip - 1], "mesh", 1)
+    weight_above = passed_along(weight[strip - 1], "mesh", 1)
+    total = element_terms(
+        jnp.concatenate([above[None], field], 0),
+        below,
+        jnp.concatenate([weight_above[None], weight], 0),
+    )
+    panel = total[1 : strip + 1, :width].reshape(node_rows, group_cols)
     rows = square_gather(panel, "c")
     cols = ring_gather(snapshots, "r")
     relayed_row, relayed_col = len(rows) - 1, len(cols) // 2

time: 191 us -> 189 us (0.990)
  waiting for transfers between devices: 105 us -> 109 us
  starting transfers between devices: 26.7 us -> 23.1 us
  other arithmetic: 4.03 us -> 6.86 us
  matrix products: 27.1 us -> 24.8 us
  local copies, waits for them, and re-layouts: 8.92 us -> 6.91 us
    ppermute x1, waiting for transfers between devices: 16.8 us -> 41.4 us  [square_gather(): z_low = lax.ppermute(block[:half], axis, to_z)]
    ppermute x1, waiting for transfers between devices: 24.2 us -> 0.01 us  [square_gather(): z_high = lax.ppermute(block[half:], axis, to_z)]
    ppermute x1, waiting for transfers between devices: 23.7 us -> 31.2 us  [ring_gather(): right_low = lax.ppermute(block[:half], axis, down)]
    ppermute x1, waiting for transfers between devices: 19.7 us -> 15.6 us  [ring_gather(): right_high = lax.ppermute(block[half:], axis, down)]
    ppermute x2, waiting for transfers between devices: 6.36 us -> 10 us  [square_gather(): corner = [lax.ppermute(x_low, axis, to_z), lax.ppermute(z_high, axis, to_x)]]
    ppermute x1, starting transfers between devices: 6.02 us -> 3.03 us  [ring_gather(): right_low = lax.ppermute(block[:half], axis, down)]
    ppermute x1, starting transfers between devices: 0.01 us -> 2.99 us  [ring_gather(): left_low = lax.ppermute(block[:half], axis, up)]
    ppermute x2 -> x3, waiting for transfers between devices: 4.95 us -> 2.25 us  [passed_along(): lax.ppermute(value, axis, [(source, source + steps) for source in range(f...]
  transfers between devices with their start and end apart: 15 -> 16, of which waited for: 9 -> 8; matrix products, arithmetic and copies ran while one was open for 15% -> 16% of each run, Pallas kernels for 0% -> 0%
where the time goes in v6:
time: 189 us; the launch traced here: 187 us
  waiting for transfers between devices  109 us (58%)
  matrix products  24.8 us (13%)
  starting transfers between devices  23.1 us (12%)
  Pallas kernels  15 us (8%)
  local copies, waits for them, and re-layouts  6.91 us (4%)
  other arithmetic  6.86 us (4%)
    ppermute x1, waiting for transfers between devices, square_gather(): z_low = lax.ppermute(block[:half], axis, to_z)  41.4 us
    ppermute x1, waiting for transfers between devices, ring_gather(): right_low = lax.ppermute(block[:half], axis, down)  31.2 us
    dot_general x23, matrix products, contract(): lax.dot_general(left, right, (((0,), (0,)), ((), ())), precision=lax.Prec...  24.8 us
    ppermute x1, waiting for transfers between devices, ring_gather(): right_high = lax.ppermute(block[half:], axis, down)  15.6 us
    pallas_call x1, Pallas kernels, scatter_to_owners(): pl.pallas_call(functools.partial(owners_kernel, side, tiles), out_shape=j...  15 us
    ppermute x2, waiting for transfers between devices, square_gather(): corner = [lax.ppermute(x_low, axis, to_z), lax.ppermute(z_high, axis, to_x)]  10 us
    ppermute x1, waiting for transfers between devices, ring_gather(): lax.ppermute(left_low, axis, up)  8.05 us
    ppermute x3, starting transfers between devices, passed_along(): lax.ppermute(value, axis, [(source, source + steps) for source in range(f...  6.76 us
  transfers between devices with their start and end apart: 16, of which 8 were waited for; matrix products, arithmetic and copies ran while one was open for 16% of the time, Pallas kernels for 0%

profile of v6, /device:TPU:31, one launch (start us, length us, event | category | flops | bytes accessed | tf_op | source)
XLA Modules:
  0.0 186.6 jit_solution(1321585104501781065)
XLA Ops:
  0.0 2.8 %fusion.31 = (f32[1536,128]{1,0:T(8,128)}, f32[1536,128]{1,0:T(8,128)}) fusion(f32[3072,128]{1,0:T(8,128)} %param.3), kind=kLoop, calls=%fused_computation.108 | loop fusion | bytes 3145728 | tf_op jit(solution)/shard_map/slice | solution.py:77
  2.8 3.0 %collective-permute-start.3 = (f32[1536,128]{1,0:T(8,128)}, f32[1536,128]{1,0:T(8,128)S(1)}, u32[]{:S(2)}, u32[]{:S(2)}) collective-permute-start(f32[1536,128]{1,0:T(8,128)} %get-tuple-element.10), channel_id=1, source_target_pairs={{0,64},{64,128},{128,192},{192,0},{1,65},{65,129},{129,193},{193,1... | collective-permute-start | bytes 2359304 | tf_op jit(solution)/shard_map/ppermute | solution.py:77
  5.8 3.0 %collective-permute-start.8 = (f32[1536,128]{1,0:T(8,128)}, f32[1536,128]{1,0:T(8,128)S(1)}, u32[]{:S(2)}, u32[]{:S(2)}) collective-permute-start(f32[1536,128]{1,0:T(8,128)} %get-tuple-element.10), channel_id=1, source_target_pairs={{0,192},{64,0},{128,64},{192,128},{1,193},{65,1},{129,65},{193,129... | collective-permute-start | bytes 2359304 | tf_op jit(solution)/shard_map/ppermute | solution.py:80
  9.7 1.3 collective-permute-start.1
  10.9 4.2 %collective-permute-start.2 = (f32[512,128]{1,0:T(8,128)}, f32[512,128]{1,0:T(8,128)}, u32[]{:S(2)}, u32[]{:S(2)}) collective-permute-start(f32[512,128]{1,0:T(8,128)} %get-tuple-element.13), channel_id=1, source_target_pairs={{1,0},{2,1},{3,2},{4,3},{5,4},{6,5},{7,6},{8,7},{9,8},{10,9},{11,1... | collective-permute-start | bytes 786440 | tf_op jit(solution)/shard_map/ppermute | solution.py:16
  15.3 1.3 collective-permute-start
  16.6 2.2 %collective-permute-done = f32[512]{0:T(512)S(1)} collective-permute-done((f32[512]{0:T(512)S(1)}, f32[512]{0:T(512)S(1)}, u32[]{:S(2)}, u32[]{:S(2)}) %collective-permute-start) | collective-permute-done | bytes 2080 | tf_op jit(solution)/shard_map/ppermute | solution.py:16
  18.9 2.6 %collective-permute-start.6 = (f32[1536,128]{1,0:T(8,128)}, f32[1536,128]{1,0:T(8,128)S(1)}, u32[]{:S(2)}, u32[]{:S(2)}) collective-permute-start(f32[1536,128]{1,0:T(8,128)} %get-tuple-element.11), channel_id=1, source_target_pairs={{0,192},{64,0},{128,64},{192,128},{1,193},{65,1},{129,65},{193,129... | collective-permute-start | bytes 2359304 | tf_op jit(solution)/shard_map/ppermute | solution.py:78
  21.6 1.1 select_maximum_fusion
  22.7 2.4 %add_multiply_fusion.3 = (f32[7,512,128]{2,1,0:T(8,128)S(1)}, f32[7,512,128]{2,1,0:T(8,128)S(1)}, f32[7,512,128]{2,1,0:T(8,128)S(1)}) fusion(f32[8,513,128]{2,1,0:T(8,128)S(1)} %select_maximum_fusion, f32[7,512]{1,0:T(8,128)S(1)} %pad_maximum_fusion.3, f32[1,512,128]{2,1,0:T(8,128)} %bitcast.4, f32[6,512,128]{2,1,0:T(8,128)S(1)} %bitcast.97, ...), kind=kLoop, calls=%fused_computation.11 | loop fusion | flops 9633792 | bytes 11286528 | tf_op jit(solution)/shard_map/mul | solution.py:37
  25.1 1.7 add_multiply_fusion.2
  27.5 1.2 collective-permute-start.10
  28.7 1.5 convolution_bitcast_fusion.8
  30.2 31.2 %collective-permute-done.8 = f32[1536,128]{1,0:T(8,128)S(1)} collective-permute-done((f32[1536,128]{1,0:T(8,128)}, f32[1536,128]{1,0:T(8,128)S(1)}, u32[]{:S(2)}, u32[]{:S(2)}) %collective-permute-start.8) | collective-permute-done | bytes 786464 | tf_op jit(solution)/shard_map/ppermute | solution.py:80
  61.5 1.2 collective-permute-start.9
  62.8 15.6 %collective-permute-done.6 = f32[1536,128]{1,0:T(8,128)S(1)} collective-permute-done((f32[1536,128]{1,0:T(8,128)}, f32[1536,128]{1,0:T(8,128)S(1)}, u32[]{:S(2)}, u32[]{:S(2)}) %collective-permute-start.6) | collective-permute-done | bytes 786464 | tf_op jit(solution)/shard_map/ppermute | solution.py:78
  78.4 1.5 convolution_bitcast_fusion.6
  79.9 2.6 %collective-permute-start.7 = (f32[1536,128]{1,0:T(8,128)S(1)}, f32[1536,128]{1,0:T(8,128)S(1)}, u32[]{:S(2)}, u32[]{:S(2)}) collective-permute-start(f32[1536,128]{1,0:T(8,128)S(1)} %collective-permute-done.6), channel_id=1, source_target_pairs={{0,192},{64,0},{128,64},{192,128},{1,193},{65,1},{129,65},{193,129... | collective-permute-start | bytes 2359304 | tf_op jit(solution)/shard_map/ppermute | solution.py:81
  82.6 1.5 convolution_bitcast_fusion.7
  84.9 1.5 convolution_bitcast_fusion.4
  86.4 1.5 convolution_bitcast_fusion.3
  87.9 41.4 %collective-permute-done.11 = f32[1536,128]{1,0:T(8,128)S(1)} collective-permute-done((f32[1536,128]{1,0:T(8,128)S(1)}, f32[1536,128]{1,0:T(8,128)S(1)}, u32[]{:S(2)}, u32[]{:S(2)}) %collective-permute-start.11) | collective-permute-done | bytes 786464 | tf_op jit(solution)/shard_map/ppermute | solution.py:68
  129.5 1.5 convolution_bitcast_fusion.5
  130.9 1.5 convolution_bitcast_fusion.1
  132.4 1.5 convolution_bitcast_fusion
  133.9 1.2 collective-permute-start.14
  135.1 1.5 convolution_bitcast_fusion.2
  138.3 8.0 %collective-permute-done.5 = f32[1536,128]{1,0:T(8,128)S(1)} collective-permute-done((f32[1536,128]{1,0:T(8,128)S(1)}, f32[1536,128]{1,0:T(8,128)S(1)}, u32[]{:S(2)}, u32[]{:S(2)}) %collective-permute-start.5) | collective-permute-done | bytes 786464 | tf_op jit(solution)/shard_map/ppermute | solution.py:81
  149.7 4.3 %collective-permute-done.14 = f32[1536,128]{1,0:T(8,128)S(1)} collective-permute-done((f32[1536,128]{1,0:T(8,128)S(1)}, f32[1536,128]{1,0:T(8,128)S(1)}, u32[]{:S(2)}, u32[]{:S(2)}) %collective-permute-start.14) | collective-permute-done | bytes 786464 | tf_op jit(solution)/shard_map/ppermute | solution.py:69
  157.3 5.7 %collective-permute-done.13 = f32[1536,128]{1,0:T(8,128)S(1)} collective-permute-done((f32[1536,128]{1,0:T(8,128)S(1)}, f32[1536,128]{1,0:T(8,128)S(1)}, u32[]{:S(2)}, u32[]{:S(2)}) %collective-permute-start.13) | collective-permute-done | bytes 786464 | tf_op jit(solution)/shard_map/ppermute | solution.py:69
  170.1 15.0 %shard_map.37 = f32[128,128]{1,0:T(8,128)} custom-call(f32[8,128,128]{2,1,0:T(8,128)} %add_multiply_fusion.4.part_ref), custom_call_target="tpu_custom_call" | custom-call | tf_op jit(solution)/shard_map/pallas_call | solution.py:191
  185.1 1.5 copy.9
  (61 shorter events, 18.2 us)
Async XLA Ops:
  0.0 8.8 %copy-start = (f32[3072,128]{1,0:T(8,128)S(1)}, f32[3072,128]{1,0:T(8,128)}, u32[]{:S(2)}) copy-start(f32[3072,128]{1,0:T(8,128)} %param.3) | copy-start | bytes 4718596
  0.0 15.1 %copy-start.1 = (s32[6,512]{1,0:T(8,128)S(1)}, s32[6,512]{1,0:T(8,128)}, u32[]{:S(2)}) copy-start(s32[6,512]{1,0:T(8,128)} %param.4) | copy-start | bytes 36868
  0.0 15.1 %copy-start.2 = (f32[8]{0:T(128)S(1)}, f32[8]{0:T(128)}, u32[]{:S(2)}) copy-start(f32[8]{0:T(128)} %param.5) | copy-start | bytes 100
  2.8 58.7 %collective-permute-start.3 = (f32[1536,128]{1,0:T(8,128)}, f32[1536,128]{1,0:T(8,128)S(1)}, u32[]{:S(2)}, u32[]{:S(2)}) collective-permute-start(f32[1536,128]{1,0:T(8,128)} %get-tuple-element.10), channel_id=1, source_target_pairs={{0,64},{64,128},{128,192},{192,0},{1,65},{65,129},{129,193},{193,1... | collective-permute-start | bytes 2359304 | tf_op jit(solution)/shard_map/ppermute | solution.py:77
  5.8 55.7 %collective-permute-start.8 = (f32[1536,128]{1,0:T(8,128)}, f32[1536,128]{1,0:T(8,128)S(1)}, u32[]{:S(2)}, u32[]{:S(2)}) collective-permute-start(f32[1536,128]{1,0:T(8,128)} %get-tuple-element.10), channel_id=1, source_target_pairs={{0,192},{64,0},{128,64},{192,128},{1,193},{65,1},{129,65},{193,129... | collective-permute-start | bytes 2359304 | tf_op jit(solution)/shard_map/ppermute | solution.py:80
  9.7 11.9 %collective-permute-start.1 = (f32[512,128]{1,0:T(8,128)}, f32[512,128]{1,0:T(8,128)S(1)}, u32[]{:S(2)}, u32[]{:S(2)}) collective-permute-start(f32[512,128]{1,0:T(8,128)} %get-tuple-element.12), channel_id=1, source_target_pairs={{0,1},{1,2},{2,3},{3,4},{4,5},{5,6},{6,7},{7,8},{8,9},{9,10},{10,1... | collective-permute-start | bytes 786440 | tf_op jit(solution)/shard_map/ppermute | solution.py:16
  10.9 10.7 %collective-permute-start.2 = (f32[512,128]{1,0:T(8,128)}, f32[512,128]{1,0:T(8,128)}, u32[]{:S(2)}, u32[]{:S(2)}) collective-permute-start(f32[512,128]{1,0:T(8,128)} %get-tuple-element.13), channel_id=1, source_target_pairs={{1,0},{2,1},{3,2},{4,3},{5,4},{6,5},{7,6},{8,7},{9,8},{10,9},{11,1... | collective-permute-start | bytes 786440 | tf_op jit(solution)/shard_map/ppermute | solution.py:16
  15.3 3.6 %collective-permute-start = (f32[512]{0:T(512)S(1)}, f32[512]{0:T(512)S(1)}, u32[]{:S(2)}, u32[]{:S(2)}) collective-permute-start(f32[512]{0:T(512)S(1)} %bitcast.112), channel_id=1, source_target_pairs={{0,1},{1,2},{2,3},{3,4},{4,5},{5,6},{6,7},{7,8},{8,9},{9,10},{10,1... | collective-permute-start | bytes 6152 | tf_op jit(solution)/shard_map/ppermute | solution.py:16
  18.9 59.5 %collective-permute-start.6 = (f32[1536,128]{1,0:T(8,128)}, f32[1536,128]{1,0:T(8,128)S(1)}, u32[]{:S(2)}, u32[]{:S(2)}) collective-permute-start(f32[1536,128]{1,0:T(8,128)} %get-tuple-element.11), channel_id=1, source_target_pairs={{0,192},{64,0},{128,64},{192,128},{1,193},{65,1},{129,65},{193,129... | collective-permute-start | bytes 2359304 | tf_op jit(solution)/shard_map/ppermute | solution.py:78
  21.5 58.3 %collective-permute-start.4 = (f32[1536,128]{1,0:T(8,128)}, f32[1536,128]{1,0:T(8,128)S(1)}, u32[]{:S(2)}, u32[]{:S(2)}) collective-permute-start(f32[1536,128]{1,0:T(8,128)} %get-tuple-element.11), channel_id=1, source_target_pairs={{0,64},{64,128},{128,192},{192,0},{1,65},{65,129},{129,193},{193,1... | collective-permute-start | bytes 2359304 | tf_op jit(solution)/shard_map/ppermute | solution.py:79
  27.5 57.3 %collective-permute-start.10 = (f32[1536,128]{1,0:T(8,128)S(1)}, f32[1536,128]{1,0:T(8,128)S(1)}, u32[]{:S(2)}, u32[]{:S(2)}) collective-permute-start(f32[1536,128]{1,0:T(8,128)S(1)} %bitcast.102), channel_id=1, source_target_pairs={{0,16},{16,0},{32,48},{48,32},{1,17},{17,1},{33,49},{49,33},{2,18}... | collective-permute-start | bytes 2359304 | tf_op jit(solution)/shard_map/ppermute | solution.py:67
  61.4 67.9 %collective-permute-start.12 = (f32[1536,128]{1,0:T(8,128)S(1)}, f32[1536,128]{1,0:T(8,128)S(1)}, u32[]{:S(2)}, u32[]{:S(2)}) collective-permute-start(f32[1536,128]{1,0:T(8,128)S(1)} %bitcast.103), channel_id=1, source_target_pairs={{0,32},{16,48},{32,0},{48,16},{1,33},{17,49},{33,1},{49,17},{2,34}... | collective-permute-start | bytes 2359304 | tf_op jit(solution)/shard_map/ppermute | solution.py:66
  61.5 22.5 %collective-permute-start.9 = (f32[1536,128]{1,0:T(8,128)S(1)}, f32[1536,128]{1,0:T(8,128)S(1)}, u32[]{:S(2)}, u32[]{:S(2)}) collective-permute-start(f32[1536,128]{1,0:T(8,128)S(1)} %bitcast.105), channel_id=1, source_target_pairs={{0,16},{16,0},{32,48},{48,32},{1,17},{17,1},{33,49},{49,33},{2,18}... | collective-permute-start | bytes 2359304 | tf_op jit(solution)/shard_map/ppermute | solution.py:65
  78.3 51.0 %collective-permute-start.11 = (f32[1536,128]{1,0:T(8,128)S(1)}, f32[1536,128]{1,0:T(8,128)S(1)}, u32[]{:S(2)}, u32[]{:S(2)}) collective-permute-start(f32[1536,128]{1,0:T(8,128)S(1)} %bitcast.106), channel_id=1, source_target_pairs={{0,32},{16,48},{32,0},{48,16},{1,33},{17,49},{33,1},{49,17},{2,34}... | collective-permute-start | bytes 2359304 | tf_op jit(solution)/shard_map/ppermute | solution.py:68
  79.9 56.7 %collective-permute-start.7 = (f32[1536,128]{1,0:T(8,128)S(1)}, f32[1536,128]{1,0:T(8,128)S(1)}, u32[]{:S(2)}, u32[]{:S(2)}) collective-permute-start(f32[1536,128]{1,0:T(8,128)S(1)} %collective-permute-done.6), channel_id=1, source_target_pairs={{0,192},{64,0},{128,64},{192,128},{1,193},{65,1},{129,65},{193,129... | collective-permute-start | bytes 2359304 | tf_op jit(solution)/shard_map/ppermute | solution.py:81
  84.1 62.2 %collective-permute-start.5 = (f32[1536,128]{1,0:T(8,128)S(1)}, f32[1536,128]{1,0:T(8,128)S(1)}, u32[]{:S(2)}, u32[]{:S(2)}) collective-permute-start(f32[1536,128]{1,0:T(8,128)S(1)} %collective-permute-done.3), channel_id=1, source_target_pairs={{0,64},{64,128},{128,192},{192,0},{1,65},{65,129},{129,193},{193,1... | collective-permute-start | bytes 2359304 | tf_op jit(solution)/shard_map/ppermute | solution.py:81
  133.9 20.1 %collective-permute-start.14 = (f32[1536,128]{1,0:T(8,128)S(1)}, f32[1536,128]{1,0:T(8,128)S(1)}, u32[]{:S(2)}, u32[]{:S(2)}) collective-permute-start(f32[1536,128]{1,0:T(8,128)S(1)} %collective-permute-done.12), channel_id=1, source_target_pairs={{0,16},{16,0},{32,48},{48,32},{1,17},{17,1},{33,49},{49,33},{2,18}... | collective-permute-start | bytes 2359304 | tf_op jit(solution)/shard_map/ppermute | solution.py:69
  135.1 27.9 %collective-permute-start.13 = (f32[1536,128]{1,0:T(8,128)S(1)}, f32[1536,128]{1,0:T(8,128)S(1)}, u32[]{:S(2)}, u32[]{:S(2)}) collective-permute-start(f32[1536,128]{1,0:T(8,128)S(1)} %collective-permute-done.9), channel_id=1, source_target_pairs={{0,32},{16,48},{32,0},{48,16},{1,33},{17,49},{33,1},{49,17},{2,34}... | collective-permute-start | bytes 2359304 | tf_op jit(solution)/shard_map/ppermute | solution.py:69
  167.1 2.1 %collective-permute-start.15 = (f32[8,128,128]{2,1,0:T(8,128)S(1)}, f32[8,128,128]{2,1,0:T(8,128)S(1)}, u32[]{:S(2)}, u32[]{:S(2)}) collective-permute-start(f32[8,128,128]{2,1,0:T(8,128)S(1)} %gather_fusion.1), channel_id=1, source_target_pairs={{0,1},{1,0},{2,3},{3,2},{4,5},{5,4},{6,7},{7,6},{8,9},{9,8},{10,11... | collective-permute-start | bytes 1572872 | tf_op jit(solution)/shard_map/ppermute | solution.py:190

commit v7 on v6

--- a/solution.py
+++ b/solution.py
@@ -211,7 +211,9 @@
     weight = weights_of(region_ids, conductivity)
     below = passed_along(field[0], "mesh", -1)
     above = passed_along(field[strip - 1], "mesh", 1)
-    weight_above = passed_along(weight[strip - 1], "mesh", 1)
+    region_above = passed_along(region_ids[strip - 1], "mesh", 1)
+    has_above = lax.axis_index("mesh") > 0
+    weight_above = jnp.where(has_above, weights_of(region_above[None], conductivity)[0], 0.0)
     total = element_terms(
         jnp.concatenate([above[None], field], 0),
         below,

time: 189 us -> 189 us (level)
  no operation moved by 1% of the time
where the time goes in v7:
time: 189 us; the launch traced here: 187 us
  waiting for transfers between devices  109 us (58%)
  matrix products  24.8 us (13%)
  starting transfers between devices  23.1 us (12%)
  Pallas kernels  15 us (8%)
  other arithmetic  6.95 us (4%)
  local copies, waits for them, and re-layouts  6.9 us (4%)
    ppermute x1, waiting for transfers between devices, square_gather(): z_low = lax.ppermute(block[:half], axis, to_z)  41.4 us
    ppermute x1, waiting for transfers between devices, ring_gather(): right_low = lax.ppermute(block[:half], axis, down)  31.3 us
    dot_general x23, matrix products, contract(): lax.dot_general(left, right, (((0,), (0,)), ((), ())), precision=lax.Prec...  24.8 us
    ppermute x1, waiting for transfers between devices, ring_gather(): right_high = lax.ppermute(block[half:], axis, down)  15.6 us
    pallas_call x1, Pallas kernels, scatter_to_owners(): pl.pallas_call(functools.partial(owners_kernel, side, tiles), out_shape=j...  15 us
    ppermute x2, waiting for transfers between devices, square_gather(): corner = [lax.ppermute(x_low, axis, to_z), lax.ppermute(z_high, axis, to_x)]  10 us
    ppermute x1, waiting for transfers between devices, ring_gather(): lax.ppermute(left_low, axis, up)  8.05 us
    ppermute x3, starting transfers between devices, passed_along(): lax.ppermute(value, axis, [(source, source + steps) for source in range(f...  6.77 us
  transfers between devices with their start and end apart: 16, of which 8 were waited for; matrix products, arithmetic and copies ran while one was open for 16% of the time, Pallas kernels for 0%

profile of v7, /device:TPU:31, one launch (start us, length us, event | category | flops | bytes accessed | tf_op | source)
XLA Modules:
  0.0 186.6 jit_solution(17006336703346424596)
XLA Ops:
  0.0 2.8 %fusion.31 = (f32[1536,128]{1,0:T(8,128)}, f32[1536,128]{1,0:T(8,128)}) fusion(f32[3072,128]{1,0:T(8,128)} %param.3), kind=kLoop, calls=%fused_computation.111 | loop fusion | bytes 3145728 | tf_op jit(solution)/shard_map/slice | solution.py:77
  2.8 3.0 %collective-permute-start.3 = (f32[1536,128]{1,0:T(8,128)}, f32[1536,128]{1,0:T(8,128)S(1)}, u32[]{:S(2)}, u32[]{:S(2)}) collective-permute-start(f32[1536,128]{1,0:T(8,128)} %get-tuple-element.10), channel_id=1, source_target_pairs={{0,64},{64,128},{128,192},{192,0},{1,65},{65,129},{129,193},{193,1... | collective-permute-start | bytes 2359304 | tf_op jit(solution)/shard_map/ppermute | solution.py:77
  5.8 3.0 %collective-permute-start.8 = (f32[1536,128]{1,0:T(8,128)}, f32[1536,128]{1,0:T(8,128)S(1)}, u32[]{:S(2)}, u32[]{:S(2)}) collective-permute-start(f32[1536,128]{1,0:T(8,128)} %get-tuple-element.10), channel_id=1, source_target_pairs={{0,192},{64,0},{128,64},{192,128},{1,193},{65,1},{129,65},{193,129... | collective-permute-start | bytes 2359304 | tf_op jit(solution)/shard_map/ppermute | solution.py:80
  9.7 1.3 collective-permute-start.1
  10.9 4.2 %collective-permute-start.2 = (f32[512,128]{1,0:T(8,128)}, f32[512,128]{1,0:T(8,128)}, u32[]{:S(2)}, u32[]{:S(2)}) collective-permute-start(f32[512,128]{1,0:T(8,128)} %get-tuple-element.13), channel_id=1, source_target_pairs={{1,0},{2,1},{3,2},{4,3},{5,4},{6,5},{7,6},{8,7},{9,8},{10,9},{11,1... | collective-permute-start | bytes 786440 | tf_op jit(solution)/shard_map/ppermute | solution.py:16
  15.2 1.3 collective-permute-start
  16.7 2.1 %collective-permute-done = s32[512]{0:T(512)S(1)} collective-permute-done((s32[512]{0:T(512)S(1)}, s32[512]{0:T(512)S(1)}, u32[]{:S(2)}, u32[]{:S(2)}) %collective-permute-start) | collective-permute-done | bytes 2080 | tf_op jit(solution)/shard_map/ppermute | solution.py:16
  18.8 2.6 %collective-permute-start.6 = (f32[1536,128]{1,0:T(8,128)}, f32[1536,128]{1,0:T(8,128)S(1)}, u32[]{:S(2)}, u32[]{:S(2)}) collective-permute-start(f32[1536,128]{1,0:T(8,128)} %get-tuple-element.11), channel_id=1, source_target_pairs={{0,192},{64,0},{128,64},{192,128},{1,193},{65,1},{129,65},{193,129... | collective-permute-start | bytes 2359304 | tf_op jit(solution)/shard_map/ppermute | solution.py:78
  21.6 1.1 select_maximum_fusion
  22.7 2.4 %add_multiply_fusion.3 = (f32[7,512,128]{2,1,0:T(8,128)S(1)}, f32[7,512,128]{2,1,0:T(8,128)S(1)}, f32[7,512,128]{2,1,0:T(8,128)S(1)}) fusion(f32[8,513,128]{2,1,0:T(8,128)S(1)} %select_maximum_fusion, f32[7,512]{1,0:T(8,128)S(1)} %pad_maximum_fusion.3, f32[1,512,128]{2,1,0:T(8,128)} %bitcast.4, f32[6,512,128]{2,1,0:T(8,128)S(1)} %bitcast.97, ...), kind=kLoop, calls=%fused_computation.11 | loop fusion | flops 9633792 | bytes 11286528 | tf_op jit(solution)/shard_map/mul | solution.py:37
  25.1 1.7 add_multiply_fusion.2
  27.5 1.2 collective-permute-start.10
  28.7 1.5 convolution_bitcast_fusion.8
  30.2 31.3 %collective-permute-done.8 = f32[1536,128]{1,0:T(8,128)S(1)} collective-permute-done((f32[1536,128]{1,0:T(8,128)}, f32[1536,128]{1,0:T(8,128)S(1)}, u32[]{:S(2)}, u32[]{:S(2)}) %collective-permute-start.8) | collective-permute-done | bytes 786464 | tf_op jit(solution)/shard_map/ppermute | solution.py:80
  61.5 1.2 collective-permute-start.9
  62.8 15.6 %collective-permute-done.6 = f32[1536,128]{1,0:T(8,128)S(1)} collective-permute-done((f32[1536,128]{1,0:T(8,128)}, f32[1536,128]{1,0:T(8,128)S(1)}, u32[]{:S(2)}, u32[]{:S(2)}) %collective-permute-start.6) | collective-permute-done | bytes 786464 | tf_op jit(solution)/shard_map/ppermute | solution.py:78
  78.4 1.5 convolution_bitcast_fusion.6
  79.9 2.6 %collective-permute-start.7 = (f32[1536,128]{1,0:T(8,128)S(1)}, f32[1536,128]{1,0:T(8,128)S(1)}, u32[]{:S(2)}, u32[]{:S(2)}) collective-permute-start(f32[1536,128]{1,0:T(8,128)S(1)} %collective-permute-done.6), channel_id=1, source_target_pairs={{0,192},{64,0},{128,64},{192,128},{1,193},{65,1},{129,65},{193,129... | collective-permute-start | bytes 2359304 | tf_op jit(solution)/shard_map/ppermute | solution.py:81
  82.6 1.5 convolution_bitcast_fusion.7
  84.9 1.5 convolution_bitcast_fusion.4
  86.4 1.5 convolution_bitcast_fusion.3
  87.9 41.4 %collective-permute-done.11 = f32[1536,128]{1,0:T(8,128)S(1)} collective-permute-done((f32[1536,128]{1,0:T(8,128)S(1)}, f32[1536,128]{1,0:T(8,128)S(1)}, u32[]{:S(2)}, u32[]{:S(2)}) %collective-permute-start.11) | collective-permute-done | bytes 786464 | tf_op jit(solution)/shard_map/ppermute | solution.py:68
  129.5 1.5 convolution_bitcast_fusion.5
  130.9 1.5 convolution_bitcast_fusion.1
  132.4 1.5 convolution_bitcast_fusion
  133.9 1.2 collective-permute-start.14
  135.1 1.5 convolution_bitcast_fusion.2
  138.3 8.1 %collective-permute-done.5 = f32[1536,128]{1,0:T(8,128)S(1)} collective-permute-done((f32[1536,128]{1,0:T(8,128)S(1)}, f32[1536,128]{1,0:T(8,128)S(1)}, u32[]{:S(2)}, u32[]{:S(2)}) %collective-permute-start.5) | collective-permute-done | bytes 786464 | tf_op jit(solution)/shard_map/ppermute | solution.py:81
  149.7 4.3 %collective-permute-done.14 = f32[1536,128]{1,0:T(8,128)S(1)} collective-permute-done((f32[1536,128]{1,0:T(8,128)S(1)}, f32[1536,128]{1,0:T(8,128)S(1)}, u32[]{:S(2)}, u32[]{:S(2)}) %collective-permute-start.14) | collective-permute-done | bytes 786464 | tf_op jit(solution)/shard_map/ppermute | solution.py:69
  157.3 5.7 %collective-permute-done.13 = f32[1536,128]{1,0:T(8,128)S(1)} collective-permute-done((f32[1536,128]{1,0:T(8,128)S(1)}, f32[1536,128]{1,0:T(8,128)S(1)}, u32[]{:S(2)}, u32[]{:S(2)}) %collective-permute-start.13) | collective-permute-done | bytes 786464 | tf_op jit(solution)/shard_map/ppermute | solution.py:69
  170.1 15.0 %shard_map.37 = f32[128,128]{1,0:T(8,128)} custom-call(f32[8,128,128]{2,1,0:T(8,128)} %add_multiply_fusion.4.part_ref), custom_call_target="tpu_custom_call" | custom-call | tf_op jit(solution)/shard_map/pallas_call | solution.py:191
  185.1 1.5 copy.9
  (63 shorter events, 18.3 us)
Async XLA Ops:
  0.0 8.8 %copy-start = (f32[3072,128]{1,0:T(8,128)S(1)}, f32[3072,128]{1,0:T(8,128)}, u32[]{:S(2)}) copy-start(f32[3072,128]{1,0:T(8,128)} %param.3) | copy-start | bytes 4718596
  0.0 15.1 %copy-start.1 = (s32[6,512]{1,0:T(8,128)S(1)}, s32[6,512]{1,0:T(8,128)}, u32[]{:S(2)}) copy-start(s32[6,512]{1,0:T(8,128)} %param.4) | copy-start | bytes 36868
  0.0 16.5 %copy-start.2 = (f32[8]{0:T(128)S(1)}, f32[8]{0:T(128)}, u32[]{:S(2)}) copy-start(f32[8]{0:T(128)} %param.5) | copy-start | bytes 100
  2.8 58.7 %collective-permute-start.3 = (f32[1536,128]{1,0:T(8,128)}, f32[1536,128]{1,0:T(8,128)S(1)}, u32[]{:S(2)}, u32[]{:S(2)}) collective-permute-start(f32[1536,128]{1,0:T(8,128)} %get-tuple-element.10), channel_id=1, source_target_pairs={{0,64},{64,128},{128,192},{192,0},{1,65},{65,129},{129,193},{193,1... | collective-permute-start | bytes 2359304 | tf_op jit(solution)/shard_map/ppermute | solution.py:77
  5.8 55.7 %collective-permute-start.8 = (f32[1536,128]{1,0:T(8,128)}, f32[1536,128]{1,0:T(8,128)S(1)}, u32[]{:S(2)}, u32[]{:S(2)}) collective-permute-start(f32[1536,128]{1,0:T(8,128)} %get-tuple-element.10), channel_id=1, source_target_pairs={{0,192},{64,0},{128,64},{192,128},{1,193},{65,1},{129,65},{193,129... | collective-permute-start | bytes 2359304 | tf_op jit(solution)/shard_map/ppermute | solution.py:80
  9.7 11.8 %collective-permute-start.1 = (f32[512,128]{1,0:T(8,128)}, f32[512,128]{1,0:T(8,128)S(1)}, u32[]{:S(2)}, u32[]{:S(2)}) collective-permute-start(f32[512,128]{1,0:T(8,128)} %get-tuple-element.12), channel_id=1, source_target_pairs={{0,1},{1,2},{2,3},{3,4},{4,5},{5,6},{6,7},{7,8},{8,9},{9,10},{10,1... | collective-permute-start | bytes 786440 | tf_op jit(solution)/shard_map/ppermute | solution.py:16
  10.9 10.7 %collective-permute-start.2 = (f32[512,128]{1,0:T(8,128)}, f32[512,128]{1,0:T(8,128)}, u32[]{:S(2)}, u32[]{:S(2)}) collective-permute-start(f32[512,128]{1,0:T(8,128)} %get-tuple-element.13), channel_id=1, source_target_pairs={{1,0},{2,1},{3,2},{4,3},{5,4},{6,5},{7,6},{8,7},{9,8},{10,9},{11,1... | collective-permute-start | bytes 786440 | tf_op jit(solution)/shard_map/ppermute | solution.py:16
  15.2 3.6 %collective-permute-start = (s32[512]{0:T(512)S(1)}, s32[512]{0:T(512)S(1)}, u32[]{:S(2)}, u32[]{:S(2)}) collective-permute-start(s32[512]{0:T(512)S(1)} %bitcast.112), channel_id=1, source_target_pairs={{0,1},{1,2},{2,3},{3,4},{4,5},{5,6},{6,7},{7,8},{8,9},{9,10},{10,1... | collective-permute-start | bytes 6152 | tf_op jit(solution)/shard_map/ppermute | solution.py:16
  18.8 59.6 %collective-permute-start.6 = (f32[1536,128]{1,0:T(8,128)}, f32[1536,128]{1,0:T(8,128)S(1)}, u32[]{:S(2)}, u32[]{:S(2)}) collective-permute-start(f32[1536,128]{1,0:T(8,128)} %get-tuple-element.11), channel_id=1, source_target_pairs={{0,192},{64,0},{128,64},{192,128},{1,193},{65,1},{129,65},{193,129... | collective-permute-start | bytes 2359304 | tf_op jit(solution)/shard_map/ppermute | solution.py:78
  21.5 58.4 %collective-permute-start.4 = (f32[1536,128]{1,0:T(8,128)}, f32[1536,128]{1,0:T(8,128)S(1)}, u32[]{:S(2)}, u32[]{:S(2)}) collective-permute-start(f32[1536,128]{1,0:T(8,128)} %get-tuple-element.11), channel_id=1, source_target_pairs={{0,64},{64,128},{128,192},{192,0},{1,65},{65,129},{129,193},{193,1... | collective-permute-start | bytes 2359304 | tf_op jit(solution)/shard_map/ppermute | solution.py:79
  27.5 57.4 %collective-permute-start.10 = (f32[1536,128]{1,0:T(8,128)S(1)}, f32[1536,128]{1,0:T(8,128)S(1)}, u32[]{:S(2)}, u32[]{:S(2)}) collective-permute-start(f32[1536,128]{1,0:T(8,128)S(1)} %bitcast.102), channel_id=1, source_target_pairs={{0,16},{16,0},{32,48},{48,32},{1,17},{17,1},{33,49},{49,33},{2,18}... | collective-permute-start | bytes 2359304 | tf_op jit(solution)/shard_map/ppermute | solution.py:67
  61.4 67.9 %collective-permute-start.12 = (f32[1536,128]{1,0:T(8,128)S(1)}, f32[1536,128]{1,0:T(8,128)S(1)}, u32[]{:S(2)}, u32[]{:S(2)}) collective-permute-start(f32[1536,128]{1,0:T(8,128)S(1)} %bitcast.103), channel_id=1, source_target_pairs={{0,32},{16,48},{32,0},{48,16},{1,33},{17,49},{33,1},{49,17},{2,34}... | collective-permute-start | bytes 2359304 | tf_op jit(solution)/shard_map/ppermute | solution.py:66
  61.5 22.5 %collective-permute-start.9 = (f32[1536,128]{1,0:T(8,128)S(1)}, f32[1536,128]{1,0:T(8,128)S(1)}, u32[]{:S(2)}, u32[]{:S(2)}) collective-permute-start(f32[1536,128]{1,0:T(8,128)S(1)} %bitcast.105), channel_id=1, source_target_pairs={{0,16},{16,0},{32,48},{48,32},{1,17},{17,1},{33,49},{49,33},{2,18}... | collective-permute-start | bytes 2359304 | tf_op jit(solution)/shard_map/ppermute | solution.py:65
  78.3 51.0 %collective-permute-start.11 = (f32[1536,128]{1,0:T(8,128)S(1)}, f32[1536,128]{1,0:T(8,128)S(1)}, u32[]{:S(2)}, u32[]{:S(2)}) collective-permute-start(f32[1536,128]{1,0:T(8,128)S(1)} %bitcast.106), channel_id=1, source_target_pairs={{0,32},{16,48},{32,0},{48,16},{1,33},{17,49},{33,1},{49,17},{2,34}... | collective-permute-start | bytes 2359304 | tf_op jit(solution)/shard_map/ppermute | solution.py:68
  79.9 56.7 %collective-permute-start.7 = (f32[1536,128]{1,0:T(8,128)S(1)}, f32[1536,128]{1,0:T(8,128)S(1)}, u32[]{:S(2)}, u32[]{:S(2)}) collective-permute-start(f32[1536,128]{1,0:T(8,128)S(1)} %collective-permute-done.6), channel_id=1, source_target_pairs={{0,192},{64,0},{128,64},{192,128},{1,193},{65,1},{129,65},{193,129... | collective-permute-start | bytes 2359304 | tf_op jit(solution)/shard_map/ppermute | solution.py:81
  84.1 62.2 %collective-permute-start.5 = (f32[1536,128]{1,0:T(8,128)S(1)}, f32[1536,128]{1,0:T(8,128)S(1)}, u32[]{:S(2)}, u32[]{:S(2)}) collective-permute-start(f32[1536,128]{1,0:T(8,128)S(1)} %collective-permute-done.3), channel_id=1, source_target_pairs={{0,64},{64,128},{128,192},{192,0},{1,65},{65,129},{129,193},{193,1... | collective-permute-start | bytes 2359304 | tf_op jit(solution)/shard_map/ppermute | solution.py:81
  133.9 20.1 %collective-permute-start.14 = (f32[1536,128]{1,0:T(8,128)S(1)}, f32[1536,128]{1,0:T(8,128)S(1)}, u32[]{:S(2)}, u32[]{:S(2)}) collective-permute-start(f32[1536,128]{1,0:T(8,128)S(1)} %collective-permute-done.12), channel_id=1, source_target_pairs={{0,16},{16,0},{32,48},{48,32},{1,17},{17,1},{33,49},{49,33},{2,18}... | collective-permute-start | bytes 2359304 | tf_op jit(solution)/shard_map/ppermute | solution.py:69
  135.1 27.9 %collective-permute-start.13 = (f32[1536,128]{1,0:T(8,128)S(1)}, f32[1536,128]{1,0:T(8,128)S(1)}, u32[]{:S(2)}, u32[]{:S(2)}) collective-permute-start(f32[1536,128]{1,0:T(8,128)S(1)} %collective-permute-done.9), channel_id=1, source_target_pairs={{0,32},{16,48},{32,0},{48,16},{1,33},{17,49},{33,1},{49,17},{2,34}... | collective-permute-start | bytes 2359304 | tf_op jit(solution)/shard_map/ppermute | solution.py:69
  167.1 2.1 %collective-permute-start.15 = (f32[8,128,128]{2,1,0:T(8,128)S(1)}, f32[8,128,128]{2,1,0:T(8,128)S(1)}, u32[]{:S(2)}, u32[]{:S(2)}) collective-permute-start(f32[8,128,128]{2,1,0:T(8,128)S(1)} %gather_fusion.1), channel_id=1, source_target_pairs={{0,1},{1,0},{2,3},{3,2},{4,5},{5,4},{6,7},{7,6},{8,9},{9,8},{10,11... | collective-permute-start | bytes 1572872 | tf_op jit(solution)/shard_map/ppermute | solution.py:190
